TPU v7x, 256 devices: a whole 4x4x8 slice. The times are simulated.
256 devices in a mesh: lx: 8 (over z), ly: 8 (over x, y_lo), blk: 4 (over y_hi, core).
Axes of the slice: x: 4, y: 4 (y_hi: 2, y_lo: 2; y = y_hi * 2 + y_lo), z: 8, core: 2. Of those that a mesh axis runs over, the one named last changes fastest.
Arguments:
- block_vectors: float32 [32, 1024, 2048], P('blk', 'lx', 'ly'), may hold values from -6 to 6
- search_vectors: float32 [256, 1024, 2048], P('blk', 'lx', 'ly'), may hold values from -6 to 6
- onsite_energy: float32 [1024, 2048], P('lx', 'ly'), may hold values from -1 to 1
- site_mask: int32 [1024, 2048], P('lx', 'ly'), may hold values 0 or 1
- filter_coefs: float32 [5], replicated, may hold values from -1 to 1
Outputs:
- projected: float32 [2, 32, 256], P(None, None, 'blk')
Inputs may be any that keep to these rules, and one draw needn't show every extreme that they name: `site_mask`: 1 marks a present site, 0 a vacancy.
All inputs are finite; a program needn't handle non-finite values. No bound on the sum of `site_mask` on one device may be relied on, other than what follows from the above.
Results may differ from a plain program's by a relative error of at most 0.00016.
Values sent between devices are 32-bit elements; how exact they have to be, the bound alone decides.
No kernel may reach another device: no remote copies, remote signals or barrier semaphores. Data moves between devices by JAX's collectives and lax.ppermute only.
A program may use at most 64 MiB of HBM per device.

v0:
```python
import math

import jax
import jax.numpy as jnp
from jax import lax
from jax.sharding import PartitionSpec as P


def extended(block, sides, width):
    for axis, dim in sides:
        count = lax.axis_size(axis)
        forward = [(i, i + 1) for i in range(count - 1)]
        backward = [(target, source) for source, target in forward]
        low = lax.ppermute(
            lax.slice_in_dim(block, block.shape[dim] - width, None, axis=dim), axis, forward
        )
        high = lax.ppermute(lax.slice_in_dim(block, 0, width, axis=dim), axis, backward)
        block = jnp.concatenate([low, block, high], axis=dim)
    return block


def scaled_step(padded, onsite, present):
    nrows, ncols = onsite.shape
    row_index = lax.broadcasted_iota(jnp.int32, (nrows, ncols), 0)
    col_index = lax.broadcasted_iota(jnp.int32, (nrows, ncols), 1)
    even_sites = (row_index + col_index) % 2 == 0
    centre = padded[..., 1:-1, 1:-1]
    left_side = padded[..., 1:-1, :-2]
    right_side = padded[..., 1:-1, 2:]
    upper_side = padded[..., :-2, 1:-1]
    lower_side = padded[..., 2:, 1:-1]
    vertical = jnp.where(even_sites, lower_side, upper_side)
    return present * (onsite * centre - (left_side + right_side + vertical)) * 0.25


def gram_rows(stacked, search_vectors):
    stacks, members, nrows, ncols = stacked.shape
    flat = stacked.reshape(stacks * members, nrows * ncols)
    search_flat = search_vectors.reshape(search_vectors.shape[0], nrows * ncols)
    result = lax.dot_general(
        flat,
        search_flat,
        (((1,), (1,)), ((), ())),
        precision=lax.Precision.HIGHEST,
        preferred_element_type=jnp.float32,
    )
    return result.reshape(stacks, members, search_vectors.shape[0])


def shards(block_vectors, search_vectors, onsite_energy, site_mask, filter_coefs):
    present = site_mask.astype(jnp.float32)
    current = block_vectors * present
    filtered = filter_coefs[0] * current
    degree = filter_coefs.shape[0] - 1
    before = current
    for order in range(1, degree + 1):
        padded_field = extended(current, (("lx", 1), ("ly", 2)), 1)
        image = scaled_step(padded_field, onsite_energy, present)
        following = image if order == 1 else 2.0 * image - before
        before, current = (current, following)
        filtered = filtered + filter_coefs[order] * current
    nrows, ncols = onsite_energy.shape
    scale_factor = 1.0 / math.sqrt(nrows * ncols * lax.axis_size("lx") * lax.axis_size("ly"))
    padded_field = extended(filtered, (("lx", 1), ("ly", 2)), 1)
    image = scaled_step(padded_field, onsite_energy, present)
    paired = jnp.stack([filtered, image])
    partial_gram = gram_rows(lax.all_gather(paired, "blk", axis=1, tiled=True), search_vectors)
    total = lax.psum(partial_gram, ("lx", "ly"))
    return total * scale_factor


def solution(mesh):
    placed = (P("blk", "lx", "ly"), P("blk", "lx", "ly"), P("lx", "ly"), P("lx", "ly"), P())
    return jax.shard_map(
        shards, mesh=mesh, in_specs=placed, out_specs=P(None, None, "blk"), check_vma=False
    )
```

profile of v0, /device:TPU:16, one launch (start us, length us, event | category | flops | bytes accessed | tf_op | source)
XLA Modules:
  0.0 537.4 jit_solution(5126460402475514423)
XLA Ops:
  7.5 1.8 copy_multiply_fusion
  10.6 4.5 collective-permute-start
  18.8 4.5 collective-permute-start.2
  27.1 1.9 broadcast_multiply_fusion
  30.3 4.8 collective-permute-start.4
  40.6 4.8 collective-permute-start.6
  49.2 2.6 fusion.34
  53.1 4.8 collective-permute-start.8
  61.8 5.0 collective-permute-start.10
  68.8 5.0 collective-permute-done.11
  75.0 1.8 fusion.27
  78.1 4.9 collective-permute-start.12
  85.5 1.4 copy.21
  88.5 5.4 %collective-permute-start.14 = (f32[8,130,1]{1,0,2:T(8,128)S(1)}, f32[8,130,1]{1,0,2:T(8,128)S(1)}, u32[]{:S(2)}, u32[]{:S(2)}) collective-permute-start(f32[8,130,1]{1,0,2:T(8,128)S(1)} %copy.21), channel_id=1, source_target_pairs={{0,4},{4,8},{8,12},{12,16},{16,20},{20,24},{24,28},{1,5},{5,9},{9,... | collective-permute-start | bytes 12488 | tf_op jit(solution)/shard_map/ppermute | solution.py:14
  97.7 8.3 %fusion.20 = f32[8,128,256]{2,0,1:T(8,128)S(1)} fusion(f32[8,128,256]{2,0,1:T(8,128)S(1)} %fusion.34, f32[8,128,256]{2,0,1:T(8,128)} %copy-done, f32[8,1,256]{2,0,1:T(8,128)S(1)} %collective-permute-done.12, f32[8,1,256]{2,0,1:T(8,128)S(1)} %collective-permute-done.13, f32[8,130,1]{2,0,1:T(8,128)} %copy.24, f32[8,130,1]{2,0,1:T(8,128)} %copy.22, ...), kind=kLoop, calls=%fused_computation.33 | loop fusion | flops 6815744 | bytes 5562516 | tf_op jit(solution)/shard_map/add | solution.py:61
  107.3 6.0 %collective-permute-start.16 = (f32[8,1,256]{2,0,1:T(8,128)S(1)}, f32[8,1,256]{2,0,1:T(8,128)S(1)}, u32[]{:S(2)}, u32[]{:S(2)}) collective-permute-start(f32[8,1,256]{2,0,1:T(8,128)S(1)} %get-tuple-element.18), channel_id=1, source_target_pairs={{0,32},{32,64},{64,96},{96,128},{128,160},{160,192},{192,224},{1,3... | collective-permute-start | bytes 24584 | tf_op jit(solution)/shard_map/ppermute | solution.py:14
  115.3 4.8 collective-permute-start.18
  120.5 1.5 collective-permute-start.19
  122.4 4.8 collective-permute-done.19
  128.4 1.8 fusion.11
  130.2 1.5 pad_maximum_fusion
  131.7 71.7 %all-gather.2.cloned.1.call-done = f32[2,32,128,256]{3,1,2,0:T(8,128)} async-done(((f32[2,8,128,256]{3,1,2,0:T(8,128)}), f32[2,32,128,256]{3,1,2,0:T(8,128)}) %all-gather.2.cloned.1.call-update) | async-done | bytes 8388624 | tf_op jit(solution)/shard_map/all_gather | solution.py:67
  203.4 16.7 %fusion.3 = f32[2,32,64]{2,1,0:T(8,128)S(1)} fusion(f32[2,32,128,256]{3,1,2,0:T(8,128)} %all-gather.2.cloned.1.call-done, f32[64,128,256]{2,1,0:T(8,128)} %param.6), kind=kOutput, calls=%fused_computation.4 | convolution fusion | flops 1610612736 | bytes 16793600 | tf_op jit(solution)/shard_map/dot_general | solution.py:40
  220.0 309.9 %psum.7 = f32[2,32,64]{2,1,0:T(8,128)S(1)} all-reduce(f32[2,32,64]{2,1,0:T(8,128)S(1)} %fusion.3), channel_id=1, replica_groups=mesh['lx'=8,'ly'=8,'blk'=4] {'lx','ly'}, use_global_device_ids=true, to_apply=%region_0.1 | all-reduce | flops 4096 | bytes 32768 | tf_op jit(solution)/shard_map/psum | solution.py:68
  (74 shorter events, 42.6 us)
Async XLA Ops:
  6.5 196.8 %all-gather.2.cloned.1.call-start = ((), (), s32[]{:S(2)}) async-start(), calls=%async_computation | async-start | bytes 10485760 | tf_op jit(solution)/shard_map/all_gather | solution.py:67
  9.3 5.9 %collective-permute-start.1 = (f32[8,1,256]{2,0,1:T(8,128)S(1)}, f32[8,1,256]{2,0,1:T(8,128)S(1)}, u32[]{:S(2)}, u32[]{:S(2)}) collective-permute-start(f32[8,1,256]{2,0,1:T(8,128)S(1)} %get-tuple-element.25), channel_id=1, source_target_pairs={{32,0},{64,32},{96,64},{128,96},{160,128},{192,160},{224,192},{33,... | collective-permute-start | bytes 24584 | tf_op jit(solution)/shard_map/ppermute | solution.py:17
  10.6 5.9 %collective-permute-start = (f32[8,1,256]{2,0,1:T(8,128)S(1)}, f32[8,1,256]{2,0,1:T(8,128)S(1)}, u32[]{:S(2)}, u32[]{:S(2)}) collective-permute-start(f32[8,1,256]{2,0,1:T(8,128)S(1)} %get-tuple-element.26), channel_id=1, source_target_pairs={{0,32},{32,64},{64,96},{96,128},{128,160},{160,192},{192,224},{1,3... | collective-permute-start | bytes 24584 | tf_op jit(solution)/shard_map/ppermute | solution.py:14
  16.8 10.3 %copy-start.1 = (f32[128,256]{1,0:T(8,128)S(1)}, f32[128,256]{1,0:T(8,128)}, u32[]{:S(2)}) copy-start(f32[128,256]{1,0:T(8,128)} %param.7) | copy-start | bytes 393220
  17.5 8.4 %collective-permute-start.3 = (f32[8,130,1]{1,0,2:T(8,128)S(1)}, f32[8,130,1]{1,0,2:T(8,128)S(1)}, u32[]{:S(2)}, u32[]{:S(2)}) collective-permute-start(f32[8,130,1]{1,0,2:T(8,128)S(1)} %copy.11), channel_id=1, source_target_pairs={{4,0},{8,4},{12,8},{16,12},{20,16},{24,20},{28,24},{5,1},{9,5},{13... | collective-permute-start | bytes 12488 | tf_op jit(solution)/shard_map/ppermute | solution.py:17
  18.8 5.9 %collective-permute-start.2 = (f32[8,130,1]{1,0,2:T(8,128)S(1)}, f32[8,130,1]{1,0,2:T(8,128)S(1)}, u32[]{:S(2)}, u32[]{:S(2)}) collective-permute-start(f32[8,130,1]{1,0,2:T(8,128)S(1)} %copy.9), channel_id=1, source_target_pairs={{0,4},{4,8},{8,12},{12,16},{16,20},{20,24},{24,28},{1,5},{5,9},{9,... | collective-permute-start | bytes 12488 | tf_op jit(solution)/shard_map/ppermute | solution.py:14
  29.0 6.1 %collective-permute-start.5 = (f32[8,1,256]{2,0,1:T(8,128)S(1)}, f32[8,1,256]{2,0,1:T(8,128)S(1)}, u32[]{:S(2)}, u32[]{:S(2)}) collective-permute-start(f32[8,1,256]{2,0,1:T(8,128)S(1)} %get-tuple-element.23), channel_id=1, source_target_pairs={{32,0},{64,32},{96,64},{128,96},{160,128},{192,160},{224,192},{33,... | collective-permute-start | bytes 24584 | tf_op jit(solution)/shard_map/ppermute | solution.py:17
  30.3 6.2 %collective-permute-start.4 = (f32[8,1,256]{2,0,1:T(8,128)S(1)}, f32[8,1,256]{2,0,1:T(8,128)S(1)}, u32[]{:S(2)}, u32[]{:S(2)}) collective-permute-start(f32[8,1,256]{2,0,1:T(8,128)S(1)} %get-tuple-element.24), channel_id=1, source_target_pairs={{0,32},{32,64},{64,96},{96,128},{128,160},{160,192},{192,224},{1,3... | collective-permute-start | bytes 24584 | tf_op jit(solution)/shard_map/ppermute | solution.py:14
  39.3 8.7 %collective-permute-start.7 = (f32[8,130,1]{1,0,2:T(8,128)S(1)}, f32[8,130,1]{1,0,2:T(8,128)S(1)}, u32[]{:S(2)}, u32[]{:S(2)}) collective-permute-start(f32[8,130,1]{1,0,2:T(8,128)S(1)} %copy.15), channel_id=1, source_target_pairs={{4,0},{8,4},{12,8},{16,12},{20,16},{24,20},{28,24},{5,1},{9,5},{13... | collective-permute-start | bytes 12488 | tf_op jit(solution)/shard_map/ppermute | solution.py:17
  40.6 6.2 %collective-permute-start.6 = (f32[8,130,1]{1,0,2:T(8,128)S(1)}, f32[8,130,1]{1,0,2:T(8,128)S(1)}, u32[]{:S(2)}, u32[]{:S(2)}) collective-permute-start(f32[8,130,1]{1,0,2:T(8,128)S(1)} %copy.13), channel_id=1, source_target_pairs={{0,4},{4,8},{8,12},{12,16},{16,20},{20,24},{24,28},{1,5},{5,9},{9,... | collective-permute-start | bytes 12488 | tf_op jit(solution)/shard_map/ppermute | solution.py:14
  51.8 6.1 %collective-permute-start.9 = (f32[8,1,256]{2,0,1:T(8,128)S(1)}, f32[8,1,256]{2,0,1:T(8,128)S(1)}, u32[]{:S(2)}, u32[]{:S(2)}) collective-permute-start(f32[8,1,256]{2,0,1:T(8,128)S(1)} %get-tuple-element.21), channel_id=1, source_target_pairs={{32,0},{64,32},{96,64},{128,96},{160,128},{192,160},{224,192},{33,... | collective-permute-start | bytes 24584 | tf_op jit(solution)/shard_map/ppermute | solution.py:17
  53.1 6.2 %collective-permute-start.8 = (f32[8,1,256]{2,0,1:T(8,128)S(1)}, f32[8,1,256]{2,0,1:T(8,128)S(1)}, u32[]{:S(2)}, u32[]{:S(2)}) collective-permute-start(f32[8,1,256]{2,0,1:T(8,128)S(1)} %get-tuple-element.22), channel_id=1, source_target_pairs={{0,32},{32,64},{64,96},{96,128},{128,160},{160,192},{192,224},{1,3... | collective-permute-start | bytes 24584 | tf_op jit(solution)/shard_map/ppermute | solution.py:14
  61.8 6.6 %collective-permute-start.10 = (f32[8,130,1]{1,0,2:T(8,128)S(1)}, f32[8,130,1]{1,0,2:T(8,128)S(1)}, u32[]{:S(2)}, u32[]{:S(2)}) collective-permute-start(f32[8,130,1]{1,0,2:T(8,128)S(1)} %copy.17), channel_id=1, source_target_pairs={{0,4},{4,8},{8,12},{12,16},{16,20},{20,24},{24,28},{1,5},{5,9},{9,... | collective-permute-start | bytes 12488 | tf_op jit(solution)/shard_map/ppermute | solution.py:14
  67.1 6.7 %collective-permute-start.11 = (f32[8,130,1]{1,0,2:T(8,128)S(1)}, f32[8,130,1]{1,0,2:T(8,128)S(1)}, u32[]{:S(2)}, u32[]{:S(2)}) collective-permute-start(f32[8,130,1]{1,0,2:T(8,128)S(1)} %copy.19), channel_id=1, source_target_pairs={{4,0},{8,4},{12,8},{16,12},{20,16},{24,20},{28,24},{5,1},{9,5},{13... | collective-permute-start | bytes 12488 | tf_op jit(solution)/shard_map/ppermute | solution.py:17
  76.8 7.7 %copy-start = (f32[8,128,256]{2,0,1:T(8,128)}, f32[8,128,256]{2,0,1:T(8,128)S(1)}, u32[]{:S(2)}) copy-start(f32[8,128,256]{2,0,1:T(8,128)S(1)} %fusion.27) | copy-start | bytes 3145732
  76.8 6.2 %collective-permute-start.13 = (f32[8,1,256]{2,0,1:T(8,128)S(1)}, f32[8,1,256]{2,0,1:T(8,128)S(1)}, u32[]{:S(2)}, u32[]{:S(2)}) collective-permute-start(f32[8,1,256]{2,0,1:T(8,128)S(1)} %get-tuple-element.19), channel_id=1, source_target_pairs={{32,0},{64,32},{96,64},{128,96},{160,128},{192,160},{224,192},{33,... | collective-permute-start | bytes 24584 | tf_op jit(solution)/shard_map/ppermute | solution.py:17
  78.1 6.3 %collective-permute-start.12 = (f32[8,1,256]{2,0,1:T(8,128)S(1)}, f32[8,1,256]{2,0,1:T(8,128)S(1)}, u32[]{:S(2)}, u32[]{:S(2)}) collective-permute-start(f32[8,1,256]{2,0,1:T(8,128)S(1)} %get-tuple-element.20), channel_id=1, source_target_pairs={{0,32},{32,64},{64,96},{96,128},{128,160},{160,192},{192,224},{1,3... | collective-permute-start | bytes 24584 | tf_op jit(solution)/shard_map/ppermute | solution.py:14
  85.5 8.5 %copy-start.2 = (f32[5]{0:T(128)S(1)}, f32[5]{0:T(128)}, u32[]{:S(2)}) copy-start(f32[5]{0:T(128)} %param.9) | copy-start | bytes 64
  87.2 9.3 %collective-permute-start.15 = (f32[8,130,1]{1,0,2:T(8,128)S(1)}, f32[8,130,1]{1,0,2:T(8,128)S(1)}, u32[]{:S(2)}, u32[]{:S(2)}) collective-permute-start(f32[8,130,1]{1,0,2:T(8,128)S(1)} %copy.23), channel_id=1, source_target_pairs={{4,0},{8,4},{12,8},{16,12},{20,16},{24,20},{28,24},{5,1},{9,5},{13... | collective-permute-start | bytes 12488 | tf_op jit(solution)/shard_map/ppermute | solution.py:17
  88.5 6.8 %collective-permute-start.14 = (f32[8,130,1]{1,0,2:T(8,128)S(1)}, f32[8,130,1]{1,0,2:T(8,128)S(1)}, u32[]{:S(2)}, u32[]{:S(2)}) collective-permute-start(f32[8,130,1]{1,0,2:T(8,128)S(1)} %copy.21), channel_id=1, source_target_pairs={{0,4},{4,8},{8,12},{12,16},{16,20},{20,24},{24,28},{1,5},{5,9},{9,... | collective-permute-start | bytes 12488 | tf_op jit(solution)/shard_map/ppermute | solution.py:14
  106.0 7.3 %collective-permute-start.17 = (f32[8,1,256]{2,0,1:T(8,128)S(1)}, f32[8,1,256]{2,0,1:T(8,128)S(1)}, u32[]{:S(2)}, u32[]{:S(2)}) collective-permute-start(f32[8,1,256]{2,0,1:T(8,128)S(1)} %get-tuple-element.17), channel_id=1, source_target_pairs={{32,0},{64,32},{96,64},{128,96},{160,128},{192,160},{224,192},{33,... | collective-permute-start | bytes 24584 | tf_op jit(solution)/shard_map/ppermute | solution.py:17
  107.3 7.4 %collective-permute-start.16 = (f32[8,1,256]{2,0,1:T(8,128)S(1)}, f32[8,1,256]{2,0,1:T(8,128)S(1)}, u32[]{:S(2)}, u32[]{:S(2)}) collective-permute-start(f32[8,1,256]{2,0,1:T(8,128)S(1)} %get-tuple-element.18), channel_id=1, source_target_pairs={{0,32},{32,64},{64,96},{96,128},{128,160},{160,192},{192,224},{1,3... | collective-permute-start | bytes 24584 | tf_op jit(solution)/shard_map/ppermute | solution.py:14
  115.3 6.7 %collective-permute-start.18 = (f32[8,130,1]{1,0,2:T(8,128)S(1)}, f32[8,130,1]{1,0,2:T(8,128)S(1)}, u32[]{:S(2)}, u32[]{:S(2)}) collective-permute-start(f32[8,130,1]{1,0,2:T(8,128)S(1)} %copy.25), channel_id=1, source_target_pairs={{0,4},{4,8},{8,12},{12,16},{16,20},{20,24},{24,28},{1,5},{5,9},{9,... | collective-permute-start | bytes 12488 | tf_op jit(solution)/shard_map/ppermute | solution.py:14
  120.5 6.7 %collective-permute-start.19 = (f32[8,130,1]{1,0,2:T(8,128)S(1)}, f32[8,130,1]{1,0,2:T(8,128)S(1)}, u32[]{:S(2)}, u32[]{:S(2)}) collective-permute-start(f32[8,130,1]{1,0,2:T(8,128)S(1)} %copy.27), channel_id=1, source_target_pairs={{4,0},{8,4},{12,8},{16,12},{20,16},{24,20},{28,24},{5,1},{9,5},{13... | collective-permute-start | bytes 12488 | tf_op jit(solution)/shard_map/ppermute | solution.py:17
Sparse Core Ops, SparseCore 0:
  131.8 71.4 all-gather.1
where the time goes:
time: 538 us; the launch traced here: 537 us
  blocking collectives  310 us (58%)
  waiting for transfers between devices  90.3 us (17%)
  starting transfers between devices  62.9 us (12%)
  other arithmetic  22.4 us (4%)
  local copies, waits for them, and re-layouts  20.9 us (4%)
  matrix products  16.7 us (3%)
  between operations  14.3 us (3%)
    psum x1, blocking collectives, shards(): total = lax.psum(partial_gram, ('lx', 'ly'))  310 us
    all_gather x1, waiting for transfers between devices, shards(): lax.all_gather(paired, 'blk', axis=1, tiled=True)  71.7 us
    ppermute x10, starting transfers between devices, extended(): lax.ppermute(lax.slice_in_dim(block, block.shape[dim] - width, None, axis...  49.7 us
    dot_general x1, matrix products, gram_rows(): lax.dot_general(flat, search_flat, (((1,), (1,)), ((), ())), precision=la...  16.7 us
    ppermute x10, starting transfers between devices, extended(): lax.ppermute(lax.slice_in_dim(block, 0, width, axis=dim), axis, backward)  13.1 us
  transfers between devices with their start and end apart: 21, of which 11 were waited for; matrix products, arithmetic and copies ran while one was open for 1% of the time, Pallas kernels for 0%

commit v1 on v0

--- a/solution.py
+++ b/solution.py
@@ -41,10 +41,24 @@
         flat,
         search_flat,
         (((1,), (1,)), ((), ())),
-        precision=lax.Precision.HIGHEST,
+        precision=lax.Precision.HIGH,
         preferred_element_type=jnp.float32,
     )
     return result.reshape(stacks, members, search_vectors.shape[0])
+
+
+def gathered(paired):
+    far = lax.ppermute(paired, "blk", [(0, 2), (1, 3), (2, 0), (3, 1)])
+    swap = [(0, 1), (1, 0), (2, 3), (3, 2)]
+    near = lax.ppermute(paired, "blk", swap)
+    far_near = lax.ppermute(far, "blk", swap)
+    return jnp.concatenate([paired, near, far, far_near], axis=1)
+
+
+def copies_sum(partial, axis):
+    count = lax.axis_size(axis)
+    copies = jnp.broadcast_to(partial[None], (count,) + partial.shape)
+    return lax.all_to_all(copies, axis, 0, 0).sum(0)
 
 
 def shards(block_vectors, search_vectors, onsite_energy, site_mask, filter_coefs):
@@ -64,9 +78,12 @@
     padded_field = extended(filtered, (("lx", 1), ("ly", 2)), 1)
     image = scaled_step(padded_field, onsite_energy, present)
     paired = jnp.stack([filtered, image])
-    partial_gram = gram_rows(lax.all_gather(paired, "blk", axis=1, tiled=True), search_vectors)
-    total = lax.psum(partial_gram, ("lx", "ly"))
-    return total * scale_factor
+    partial_gram = gram_rows(gathered(paired), search_vectors).reshape(32, 128)
+    total = copies_sum(copies_sum(partial_gram, "ly"), "lx").reshape(2, 4, 8, 64)
+    block = lax.axis_index("blk")
+    total = jnp.where(block % 2 == 1, total[:, jnp.array([1, 0, 3, 2])], total)
+    total = jnp.where(block >= 2, total[:, jnp.array([2, 3, 0, 1])], total)
+    return total.reshape(2, 32, 64) * scale_factor
 
 
 def solution(mesh):

time: 538 us -> 227 us (0.42)
  blocking collectives: 310 us -> 11.9 us
  local copies, waits for them, and re-layouts: 20.9 us -> 47.8 us
  between operations: 14.3 us -> 1.12 us
  matrix products: 16.7 us -> 3.94 us
  waiting for transfers between devices: 90.3 us -> 79.7 us
    psum x1 -> x0, blocking collectives: 310 us -> none  [shards(): total = lax.psum(partial_gram, ('lx', 'ly'))]
    all_gather x1 -> x0, waiting for transfers between devices: 71.7 us -> none  [shards(): lax.all_gather(paired, 'blk', axis=1, tiled=True)]
    ppermute x0 -> x3, waiting for transfers between devices: none -> 35.4 us  [the longest x1 35.4 us: gathered(): far = lax.ppermute(paired, 'blk', [(0, 2), (1, 3), (2, 0), (3, 1)])]
    ppermute x10, waiting for transfers between devices: 9.85 us -> 35 us  [extended(): lax.ppermute(lax.slice_in_dim(block, 0, width, axis=dim), axis, backward)]
    unnamed x6 -> x14, local copies, waits for them, and re-layouts: 0.01 us -> 17.6 us
    dot_general x1, matrix products: 16.7 us -> 3.94 us  [gram_rows(): lax.dot_general(flat, search_flat, (((1,), (1,)), ((), ())), precision=la...]
    all_to_all x0 -> x1, blocking collectives: none -> 11.9 us  [copies_sum(): return lax.all_to_all(copies, axis, 0, 0).sum(0)]
    ppermute x10, starting transfers between devices: 49.7 us -> 40.6 us  [extended(): lax.ppermute(lax.slice_in_dim(block, block.shape[dim] - width, None, axis...]
  transfers between devices with their start and end apart: 21 -> 24, of which waited for: 11 -> 11; matrix products, arithmetic and copies ran while one was open for 1% -> 7% of each run, Pallas kernels for 0% -> 0%
where the time goes in v1:
time: 227 us; the launch traced here: 226 us
  waiting for transfers between devices  79.7 us (35%)
  starting transfers between devices  58.8 us (26%)
  local copies, waits for them, and re-layouts  47.8 us (21%)
  other arithmetic  22.8 us (10%)
  blocking collectives  11.9 us (5%)
  matrix products  3.94 us (2%)
    ppermute x10, starting transfers between devices, extended(): lax.ppermute(lax.slice_in_dim(block, block.shape[dim] - width, None, axis...  40.6 us
    ppermute x1, waiting for transfers between devices, gathered(): far = lax.ppermute(paired, 'blk', [(0, 2), (1, 3), (2, 0), (3, 1)])  35.4 us
    ppermute x10, waiting for transfers between devices, extended(): lax.ppermute(lax.slice_in_dim(block, 0, width, axis=dim), axis, backward)  35 us
    unnamed x14, local copies, waits for them, and re-layouts  17.6 us
    ppermute x10, starting transfers between devices, extended(): lax.ppermute(lax.slice_in_dim(block, 0, width, axis=dim), axis, backward)  13.1 us
    all_to_all x1, blocking collectives, copies_sum(): return lax.all_to_all(copies, axis, 0, 0).sum(0)  11.9 us
    all_to_all x1, waiting for transfers between devices, copies_sum(): return lax.all_to_all(copies, axis, 0, 0).sum(0)  9.04 us
    add x1, other arithmetic, shards(): filtered = filtered + filter_coefs[order] * current  8.3 us
  transfers between devices with their start and end apart: 24, of which 11 were waited for; matrix products, arithmetic and copies ran while one was open for 7% of the time, Pallas kernels for 0%

profile of v1, /device:TPU:16, one launch (start us, length us, event | category | flops | bytes accessed | tf_op | source)
XLA Modules:
  0.0 226.1 jit_solution(348331425956364198)
XLA Ops:
  2.8 3.8 %collective-permute-start = (f32[8,1,256]{2,0,1:T(8,128)S(1)}, f32[8,1,256]{2,0,1:T(8,128)S(1)}, u32[]{:S(2)}, u32[]{:S(2)}) collective-permute-start(f32[8,1,256]{2,0,1:T(8,128)S(1)} %get-tuple-element.26), channel_id=1, source_target_pairs={{0,32},{32,64},{64,96},{96,128},{128,160},{160,192},{192,224},{1,3... | collective-permute-start | bytes 24584 | tf_op jit(solution)/shard_map/ppermute | solution.py:14
  8.0 4.2 %collective-permute-done.1 = f32[8,1,256]{2,0,1:T(8,128)S(1)} collective-permute-done((f32[8,1,256]{2,0,1:T(8,128)S(1)}, f32[8,1,256]{2,0,1:T(8,128)S(1)}, u32[]{:S(2)}, u32[]{:S(2)}) %collective-permute-start.1) | collective-permute-done | bytes 8224 | tf_op jit(solution)/shard_map/ppermute | solution.py:17
  12.8 3.2 %collective-permute-start.2 = (f32[8,130,1]{1,0,2:T(8,128)S(1)}, f32[8,130,1]{1,0,2:T(8,128)S(1)}, u32[]{:S(2)}, u32[]{:S(2)}) collective-permute-start(f32[8,130,1]{1,0,2:T(8,128)S(1)} %copy.94), channel_id=1, source_target_pairs={{0,4},{4,8},{8,12},{12,16},{16,20},{20,24},{24,28},{1,5},{5,9},{9,... | collective-permute-start | bytes 12488 | tf_op jit(solution)/shard_map/ppermute | solution.py:14
  25.0 3.8 %collective-permute-start.4 = (f32[8,1,256]{2,0,1:T(8,128)S(1)}, f32[8,1,256]{2,0,1:T(8,128)S(1)}, u32[]{:S(2)}, u32[]{:S(2)}) collective-permute-start(f32[8,1,256]{2,0,1:T(8,128)S(1)} %get-tuple-element.24), channel_id=1, source_target_pairs={{0,32},{32,64},{64,96},{96,128},{128,160},{160,192},{192,224},{1,3... | collective-permute-start | bytes 24584 | tf_op jit(solution)/shard_map/ppermute | solution.py:14
  30.2 5.2 %collective-permute-done.5 = f32[8,1,256]{2,0,1:T(8,128)S(1)} collective-permute-done((f32[8,1,256]{2,0,1:T(8,128)S(1)}, f32[8,1,256]{2,0,1:T(8,128)S(1)}, u32[]{:S(2)}, u32[]{:S(2)}) %collective-permute-start.5) | collective-permute-done | bytes 8224 | tf_op jit(solution)/shard_map/ppermute | solution.py:17
  39.5 5.1 %collective-permute-start.6 = (f32[8,130,1]{1,0,2:T(8,128)S(1)}, f32[8,130,1]{1,0,2:T(8,128)S(1)}, u32[]{:S(2)}, u32[]{:S(2)}) collective-permute-start(f32[8,130,1]{1,0,2:T(8,128)S(1)} %copy.98), channel_id=1, source_target_pairs={{0,4},{4,8},{8,12},{12,16},{16,20},{20,24},{24,28},{1,5},{5,9},{9,... | collective-permute-start | bytes 12488 | tf_op jit(solution)/shard_map/ppermute | solution.py:14
  50.3 5.1 %collective-permute-start.8 = (f32[8,1,256]{2,0,1:T(8,128)S(1)}, f32[8,1,256]{2,0,1:T(8,128)S(1)}, u32[]{:S(2)}, u32[]{:S(2)}) collective-permute-start(f32[8,1,256]{2,0,1:T(8,128)S(1)} %get-tuple-element.22), channel_id=1, source_target_pairs={{0,32},{32,64},{64,96},{96,128},{128,160},{160,192},{192,224},{1,3... | collective-permute-start | bytes 24584 | tf_op jit(solution)/shard_map/ppermute | solution.py:14
  56.7 4.2 %collective-permute-done.9 = f32[8,1,256]{2,0,1:T(8,128)S(1)} collective-permute-done((f32[8,1,256]{2,0,1:T(8,128)S(1)}, f32[8,1,256]{2,0,1:T(8,128)S(1)}, u32[]{:S(2)}, u32[]{:S(2)}) %collective-permute-start.9) | collective-permute-done | bytes 8224 | tf_op jit(solution)/shard_map/ppermute | solution.py:17
  63.4 4.8 %collective-permute-start.10 = (f32[8,130,1]{1,0,2:T(8,128)S(1)}, f32[8,130,1]{1,0,2:T(8,128)S(1)}, u32[]{:S(2)}, u32[]{:S(2)}) collective-permute-start(f32[8,130,1]{1,0,2:T(8,128)S(1)} %copy.102), channel_id=1, source_target_pairs={{0,4},{4,8},{8,12},{12,16},{16,20},{20,24},{24,28},{1,5},{5,9},{9,... | collective-permute-start | bytes 12488 | tf_op jit(solution)/shard_map/ppermute | solution.py:14
  70.3 4.5 %collective-permute-done.11 = f32[8,130,1]{1,0,2:T(8,128)S(1)} collective-permute-done((f32[8,130,1]{1,0,2:T(8,128)S(1)}, f32[8,130,1]{1,0,2:T(8,128)S(1)}, u32[]{:S(2)}, u32[]{:S(2)}) %collective-permute-start.11) | collective-permute-done | bytes 4192 | tf_op jit(solution)/shard_map/ppermute | solution.py:17
  77.8 3.9 %collective-permute-start.12 = (f32[8,1,256]{2,0,1:T(8,128)S(1)}, f32[8,1,256]{2,0,1:T(8,128)S(1)}, u32[]{:S(2)}, u32[]{:S(2)}) collective-permute-start(f32[8,1,256]{2,0,1:T(8,128)S(1)} %get-tuple-element.20), channel_id=1, source_target_pairs={{0,32},{32,64},{64,96},{96,128},{128,160},{160,192},{192,224},{1,3... | collective-permute-start | bytes 24584 | tf_op jit(solution)/shard_map/ppermute | solution.py:14
  83.1 4.2 %collective-permute-done.13 = f32[8,1,256]{2,0,1:T(8,128)S(1)} collective-permute-done((f32[8,1,256]{2,0,1:T(8,128)S(1)}, f32[8,1,256]{2,0,1:T(8,128)S(1)}, u32[]{:S(2)}, u32[]{:S(2)}) %collective-permute-start.13) | collective-permute-done | bytes 8224 | tf_op jit(solution)/shard_map/ppermute | solution.py:17
  89.7 4.8 %collective-permute-start.14 = (f32[8,130,1]{1,0,2:T(8,128)S(1)}, f32[8,130,1]{1,0,2:T(8,128)S(1)}, u32[]{:S(2)}, u32[]{:S(2)}) collective-permute-start(f32[8,130,1]{1,0,2:T(8,128)S(1)} %copy.106), channel_id=1, source_target_pairs={{0,4},{4,8},{8,12},{12,16},{16,20},{20,24},{24,28},{1,5},{5,9},{9,... | collective-permute-start | bytes 12488 | tf_op jit(solution)/shard_map/ppermute | solution.py:14
  101.6 8.3 %fusion.14 = f32[8,128,256]{2,0,1:T(8,128)S(1)} fusion(f32[8,128,256]{2,0,1:T(8,128)S(1)} %fusion.28, f32[8,128,256]{2,0,1:T(8,128)} %copy-done, f32[8,1,256]{2,0,1:T(8,128)S(1)} %collective-permute-done.12, f32[8,1,256]{2,0,1:T(8,128)S(1)} %collective-permute-done.13, f32[8,130,1]{2,0,1:T(8,128)} %copy.109, f32[8,130,1]{2,0,1:T(8,128)} %copy.107, ...), kind=kLoop, calls=%fused_computation.32 | loop fusion | flops 6815744 | bytes 5562516 | tf_op jit(solution)/shard_map/add | solution.py:75
  114.4 4.2 %collective-permute-done.17 = f32[8,1,256]{2,0,1:T(8,128)S(1)} collective-permute-done((f32[8,1,256]{2,0,1:T(8,128)S(1)}, f32[8,1,256]{2,0,1:T(8,128)S(1)}, u32[]{:S(2)}, u32[]{:S(2)}) %collective-permute-start.17) | collective-permute-done | bytes 8224 | tf_op jit(solution)/shard_map/ppermute | solution.py:17
  124.4 3.7 %collective-permute-done.19 = f32[8,130,1]{1,0,2:T(8,128)S(1)} collective-permute-done((f32[8,130,1]{1,0,2:T(8,128)S(1)}, f32[8,130,1]{1,0,2:T(8,128)S(1)}, u32[]{:S(2)}, u32[]{:S(2)}) %collective-permute-start.19) | collective-permute-done | bytes 4192 | tf_op jit(solution)/shard_map/ppermute | solution.py:17
  129.9 35.4 %collective-permute-done.21 = f32[2,8,128,256]{3,1,2,0:T(8,128)S(1)} collective-permute-done((f32[2,8,128,256]{3,1,2,0:T(8,128)S(1)}, f32[2,8,128,256]{3,1,2,0:T(8,128)S(1)}, u32[]{:S(2)}, u32[]{:S(2)}) %collective-permute-start.21) | collective-permute-done | bytes 2097184 | tf_op jit(solution)/shard_map/ppermute | solution.py:51
  165.3 8.1 %copy.119 = f32[8,8,128,256]{3,1,2,0:T(8,128)S(1)} copy(f32[8,8,128,256]{3,2,1,0:T(8,128)} %bitcast.35) | data formatting | bytes 16777216
  177.6 8.1 %copy.114 = f32[2,32,128,256]{3,2,1,0:T(8,128)} copy(f32[2,32,128,256]{3,1,2,0:T(8,128)S(1)} %pad_maximum_fusion) | data formatting | bytes 16777216 | tf_op jit(solution)/shard_map/concatenate | solution.py:55
  185.7 8.1 %copy.118 = f32[8,8,128,256]{3,1,2,0:T(8,128)S(1)} copy(f32[8,8,128,256]{3,2,1,0:T(8,128)} %bitcast.32) | data formatting | bytes 16777216
  193.9 3.9 %fusion.54 = f32[64,64]{1,0:T(8,128)S(1)} fusion(f32[64,32768]{1,0:T(8,128)S(1)} %bitcast.31, f32[64,32768]{1,0:T(8,128)S(1)} %bitcast.30), kind=kOutput, calls=%fused_computation.112 | convolution fusion | flops 805306368 | bytes 16793600 | tf_op jit(solution)/shard_map/dot_general | solution.py:40
  197.9 11.9 %all_to_all.10 = f32[8,32,128]{2,1,0:T(8,128)S(1)} all-to-all(f32[8,32,128]{2,1,0:T(8,128)S(1)} %broadcast_in_dim.48), channel_id=1, replica_groups=mesh['lx'=8,'ly'=8,'blk'=4] {'ly'}, dimensions={0} | all-to-all | bytes 262144 | tf_op jit(solution)/shard_map/all_to_all | solution.py:61
  210.5 4.7 %all-to-all-start.1 = ((f32[8,32,128]{2,1,0:T(8,128)}), f32[8,32,128]{2,1,0:T(8,128)S(1)}, u32[]{:S(2)}, u32[]{:S(2)}) async-start(f32[8,32,128]{2,1,0:T(8,128)} %broadcast_in_dim.49), calls=%async_computation.1 | async-start | bytes 262144 | tf_op jit(solution)/shard_map/all_to_all | solution.py:61
  215.2 9.0 %all-to-all-done.1 = f32[8,32,128]{2,1,0:T(8,128)S(1)} async-done(((f32[8,32,128]{2,1,0:T(8,128)}), f32[8,32,128]{2,1,0:T(8,128)S(1)}, u32[]{:S(2)}, u32[]{:S(2)}) %all-to-all-start.1) | async-done | bytes 131104 | tf_op jit(solution)/shard_map/all_to_all | solution.py:61
  (101 shorter events, 62.5 us)
Async XLA Ops:
  2.8 5.2 %collective-permute-start = (f32[8,1,256]{2,0,1:T(8,128)S(1)}, f32[8,1,256]{2,0,1:T(8,128)S(1)}, u32[]{:S(2)}, u32[]{:S(2)}) collective-permute-start(f32[8,1,256]{2,0,1:T(8,128)S(1)} %get-tuple-element.26), channel_id=1, source_target_pairs={{0,32},{32,64},{64,96},{96,128},{128,160},{160,192},{192,224},{1,3... | collective-permute-start | bytes 24584 | tf_op jit(solution)/shard_map/ppermute | solution.py:14
  6.6 5.5 %collective-permute-start.1 = (f32[8,1,256]{2,0,1:T(8,128)S(1)}, f32[8,1,256]{2,0,1:T(8,128)S(1)}, u32[]{:S(2)}, u32[]{:S(2)}) collective-permute-start(f32[8,1,256]{2,0,1:T(8,128)S(1)} %get-tuple-element.25), channel_id=1, source_target_pairs={{32,0},{64,32},{96,64},{128,96},{160,128},{192,160},{224,192},{33,... | collective-permute-start | bytes 24584 | tf_op jit(solution)/shard_map/ppermute | solution.py:17
  12.8 4.9 %collective-permute-start.2 = (f32[8,130,1]{1,0,2:T(8,128)S(1)}, f32[8,130,1]{1,0,2:T(8,128)S(1)}, u32[]{:S(2)}, u32[]{:S(2)}) collective-permute-start(f32[8,130,1]{1,0,2:T(8,128)S(1)} %copy.94), channel_id=1, source_target_pairs={{0,4},{4,8},{8,12},{12,16},{16,20},{20,24},{24,28},{1,5},{5,9},{9,... | collective-permute-start | bytes 12488 | tf_op jit(solution)/shard_map/ppermute | solution.py:14
  16.3 5.5 %collective-permute-start.3 = (f32[8,130,1]{1,0,2:T(8,128)S(1)}, f32[8,130,1]{1,0,2:T(8,128)S(1)}, u32[]{:S(2)}, u32[]{:S(2)}) collective-permute-start(f32[8,130,1]{1,0,2:T(8,128)S(1)} %copy.96), channel_id=1, source_target_pairs={{4,0},{8,4},{12,8},{16,12},{20,16},{24,20},{28,24},{5,1},{9,5},{13... | collective-permute-start | bytes 12488 | tf_op jit(solution)/shard_map/ppermute | solution.py:17
  25.0 5.2 %collective-permute-start.4 = (f32[8,1,256]{2,0,1:T(8,128)S(1)}, f32[8,1,256]{2,0,1:T(8,128)S(1)}, u32[]{:S(2)}, u32[]{:S(2)}) collective-permute-start(f32[8,1,256]{2,0,1:T(8,128)S(1)} %get-tuple-element.24), channel_id=1, source_target_pairs={{0,32},{32,64},{64,96},{96,128},{128,160},{160,192},{192,224},{1,3... | collective-permute-start | bytes 24584 | tf_op jit(solution)/shard_map/ppermute | solution.py:14
  28.9 6.6 %collective-permute-start.5 = (f32[8,1,256]{2,0,1:T(8,128)S(1)}, f32[8,1,256]{2,0,1:T(8,128)S(1)}, u32[]{:S(2)}, u32[]{:S(2)}) collective-permute-start(f32[8,1,256]{2,0,1:T(8,128)S(1)} %get-tuple-element.23), channel_id=1, source_target_pairs={{32,0},{64,32},{96,64},{128,96},{160,128},{192,160},{224,192},{33,... | collective-permute-start | bytes 24584 | tf_op jit(solution)/shard_map/ppermute | solution.py:17
  37.8 7.4 %collective-permute-start.7 = (f32[8,130,1]{1,0,2:T(8,128)S(1)}, f32[8,130,1]{1,0,2:T(8,128)S(1)}, u32[]{:S(2)}, u32[]{:S(2)}) collective-permute-start(f32[8,130,1]{1,0,2:T(8,128)S(1)} %copy.100), channel_id=1, source_target_pairs={{4,0},{8,4},{12,8},{16,12},{20,16},{24,20},{28,24},{5,1},{9,5},{13... | collective-permute-start | bytes 12488 | tf_op jit(solution)/shard_map/ppermute | solution.py:17
  39.5 7.0 %collective-permute-start.6 = (f32[8,130,1]{1,0,2:T(8,128)S(1)}, f32[8,130,1]{1,0,2:T(8,128)S(1)}, u32[]{:S(2)}, u32[]{:S(2)}) collective-permute-start(f32[8,130,1]{1,0,2:T(8,128)S(1)} %copy.98), channel_id=1, source_target_pairs={{0,4},{4,8},{8,12},{12,16},{16,20},{20,24},{24,28},{1,5},{5,9},{9,... | collective-permute-start | bytes 12488 | tf_op jit(solution)/shard_map/ppermute | solution.py:14
  50.3 6.5 %collective-permute-start.8 = (f32[8,1,256]{2,0,1:T(8,128)S(1)}, f32[8,1,256]{2,0,1:T(8,128)S(1)}, u32[]{:S(2)}, u32[]{:S(2)}) collective-permute-start(f32[8,1,256]{2,0,1:T(8,128)S(1)} %get-tuple-element.22), channel_id=1, source_target_pairs={{0,32},{32,64},{64,96},{96,128},{128,160},{160,192},{192,224},{1,3... | collective-permute-start | bytes 24584 | tf_op jit(solution)/shard_map/ppermute | solution.py:14
  55.4 5.5 %collective-permute-start.9 = (f32[8,1,256]{2,0,1:T(8,128)S(1)}, f32[8,1,256]{2,0,1:T(8,128)S(1)}, u32[]{:S(2)}, u32[]{:S(2)}) collective-permute-start(f32[8,1,256]{2,0,1:T(8,128)S(1)} %get-tuple-element.21), channel_id=1, source_target_pairs={{32,0},{64,32},{96,64},{128,96},{160,128},{192,160},{224,192},{33,... | collective-permute-start | bytes 24584 | tf_op jit(solution)/shard_map/ppermute | solution.py:17
  63.4 6.5 %collective-permute-start.10 = (f32[8,130,1]{1,0,2:T(8,128)S(1)}, f32[8,130,1]{1,0,2:T(8,128)S(1)}, u32[]{:S(2)}, u32[]{:S(2)}) collective-permute-start(f32[8,130,1]{1,0,2:T(8,128)S(1)} %copy.102), channel_id=1, source_target_pairs={{0,4},{4,8},{8,12},{12,16},{16,20},{20,24},{24,28},{1,5},{5,9},{9,... | collective-permute-start | bytes 12488 | tf_op jit(solution)/shard_map/ppermute | solution.py:14
  68.6 6.2 %collective-permute-start.11 = (f32[8,130,1]{1,0,2:T(8,128)S(1)}, f32[8,130,1]{1,0,2:T(8,128)S(1)}, u32[]{:S(2)}, u32[]{:S(2)}) collective-permute-start(f32[8,130,1]{1,0,2:T(8,128)S(1)} %copy.104), channel_id=1, source_target_pairs={{4,0},{8,4},{12,8},{16,12},{20,16},{24,20},{28,24},{5,1},{9,5},{13... | collective-permute-start | bytes 12488 | tf_op jit(solution)/shard_map/ppermute | solution.py:17
  77.8 5.3 %collective-permute-start.12 = (f32[8,1,256]{2,0,1:T(8,128)S(1)}, f32[8,1,256]{2,0,1:T(8,128)S(1)}, u32[]{:S(2)}, u32[]{:S(2)}) collective-permute-start(f32[8,1,256]{2,0,1:T(8,128)S(1)} %get-tuple-element.20), channel_id=1, source_target_pairs={{0,32},{32,64},{64,96},{96,128},{128,160},{160,192},{192,224},{1,3... | collective-permute-start | bytes 24584 | tf_op jit(solution)/shard_map/ppermute | solution.py:14
  81.7 5.5 %collective-permute-start.13 = (f32[8,1,256]{2,0,1:T(8,128)S(1)}, f32[8,1,256]{2,0,1:T(8,128)S(1)}, u32[]{:S(2)}, u32[]{:S(2)}) collective-permute-start(f32[8,1,256]{2,0,1:T(8,128)S(1)} %get-tuple-element.19), channel_id=1, source_target_pairs={{32,0},{64,32},{96,64},{128,96},{160,128},{192,160},{224,192},{33,... | collective-permute-start | bytes 24584 | tf_op jit(solution)/shard_map/ppermute | solution.py:17
  89.7 7.8 %collective-permute-start.14 = (f32[8,130,1]{1,0,2:T(8,128)S(1)}, f32[8,130,1]{1,0,2:T(8,128)S(1)}, u32[]{:S(2)}, u32[]{:S(2)}) collective-permute-start(f32[8,130,1]{1,0,2:T(8,128)S(1)} %copy.106), channel_id=1, source_target_pairs={{0,4},{4,8},{8,12},{12,16},{16,20},{20,24},{24,28},{1,5},{5,9},{9,... | collective-permute-start | bytes 12488 | tf_op jit(solution)/shard_map/ppermute | solution.py:14
  94.9 5.5 %collective-permute-start.15 = (f32[8,130,1]{1,0,2:T(8,128)S(1)}, f32[8,130,1]{1,0,2:T(8,128)S(1)}, u32[]{:S(2)}, u32[]{:S(2)}) collective-permute-start(f32[8,130,1]{1,0,2:T(8,128)S(1)} %copy.108), channel_id=1, source_target_pairs={{4,0},{8,4},{12,8},{16,12},{20,16},{24,20},{28,24},{5,1},{9,5},{13... | collective-permute-start | bytes 12488 | tf_op jit(solution)/shard_map/ppermute | solution.py:17
  110.0 4.5 %collective-permute-start.16 = (f32[8,1,256]{2,0,1:T(8,128)S(1)}, f32[8,1,256]{2,0,1:T(8,128)S(1)}, u32[]{:S(2)}, u32[]{:S(2)}) collective-permute-start(f32[8,1,256]{2,0,1:T(8,128)S(1)} %get-tuple-element.18), channel_id=1, source_target_pairs={{0,32},{32,64},{64,96},{96,128},{128,160},{160,192},{192,224},{1,3... | collective-permute-start | bytes 24584 | tf_op jit(solution)/shard_map/ppermute | solution.py:14
  113.1 5.5 %collective-permute-start.17 = (f32[8,1,256]{2,0,1:T(8,128)S(1)}, f32[8,1,256]{2,0,1:T(8,128)S(1)}, u32[]{:S(2)}, u32[]{:S(2)}) collective-permute-start(f32[8,1,256]{2,0,1:T(8,128)S(1)} %get-tuple-element.17), channel_id=1, source_target_pairs={{32,0},{64,32},{96,64},{128,96},{160,128},{192,160},{224,192},{33,... | collective-permute-start | bytes 24584 | tf_op jit(solution)/shard_map/ppermute | solution.py:17
  119.3 4.7 %collective-permute-start.18 = (f32[8,130,1]{1,0,2:T(8,128)S(1)}, f32[8,130,1]{1,0,2:T(8,128)S(1)}, u32[]{:S(2)}, u32[]{:S(2)}) collective-permute-start(f32[8,130,1]{1,0,2:T(8,128)S(1)} %copy.110), channel_id=1, source_target_pairs={{0,4},{4,8},{8,12},{12,16},{16,20},{20,24},{24,28},{1,5},{5,9},{9,... | collective-permute-start | bytes 12488 | tf_op jit(solution)/shard_map/ppermute | solution.py:14
  122.5 5.6 %collective-permute-start.19 = (f32[8,130,1]{1,0,2:T(8,128)S(1)}, f32[8,130,1]{1,0,2:T(8,128)S(1)}, u32[]{:S(2)}, u32[]{:S(2)}) collective-permute-start(f32[8,130,1]{1,0,2:T(8,128)S(1)} %copy.112), channel_id=1, source_target_pairs={{4,0},{8,4},{12,8},{16,12},{20,16},{24,20},{28,24},{5,1},{9,5},{13... | collective-permute-start | bytes 12488 | tf_op jit(solution)/shard_map/ppermute | solution.py:17
  129.5 35.9 %collective-permute-start.21 = (f32[2,8,128,256]{3,1,2,0:T(8,128)S(1)}, f32[2,8,128,256]{3,1,2,0:T(8,128)S(1)}, u32[]{:S(2)}, u32[]{:S(2)}) collective-permute-start(f32[2,8,128,256]{3,1,2,0:T(8,128)S(1)} %pad_maximum_fusion.1), channel_id=1, source_target_pairs={{0,2},{1,3},{2,0},{3,1},{4,6},{5,7},{6,4},{7,5},{8,10},{9,11},{10,... | collective-permute-start | bytes 6291464 | tf_op jit(solution)/shard_map/ppermute | solution.py:51
  129.9 43.6 %collective-permute-start.20 = (f32[2,8,128,256]{3,1,2,0:T(8,128)S(1)}, f32[2,8,128,256]{3,1,2,0:T(8,128)S(1)}, u32[]{:S(2)}, u32[]{:S(2)}) collective-permute-start(f32[2,8,128,256]{3,1,2,0:T(8,128)S(1)} %pad_maximum_fusion.1), channel_id=1, source_target_pairs={{0,1},{1,0},{2,3},{3,2},{4,5},{5,4},{6,7},{7,6},{8,9},{9,8},{10,11... | collective-permute-start | bytes 6291464 | tf_op jit(solution)/shard_map/ppermute | solution.py:53
  165.3 9.5 %collective-permute-start.22 = (f32[2,8,128,256]{3,1,2,0:T(8,128)S(1)}, f32[2,8,128,256]{3,1,2,0:T(8,128)}, u32[]{:S(2)}, u32[]{:S(2)}) collective-permute-start(f32[2,8,128,256]{3,1,2,0:T(8,128)S(1)} %collective-permute-done.21), channel_id=1, source_target_pairs={{0,1},{1,0},{2,3},{3,2},{4,5},{5,4},{6,7},{7,6},{8,9},{9,8},{10,11... | collective-permute-start | bytes 6291464 | tf_op jit(solution)/shard_map/ppermute | solution.py:54
  210.5 13.7 %all-to-all-start.1 = ((f32[8,32,128]{2,1,0:T(8,128)}), f32[8,32,128]{2,1,0:T(8,128)S(1)}, u32[]{:S(2)}, u32[]{:S(2)}) async-start(f32[8,32,128]{2,1,0:T(8,128)} %broadcast_in_dim.49), calls=%async_computation.1 | async-start | bytes 262144 | tf_op jit(solution)/shard_map/all_to_all | solution.py:61
  (6 other events, 72.0 us)

commit v2 on v0

v2 whole, which is shorter than its diff:
```python
import math

import jax
import jax.numpy as jnp
from jax import lax
from jax.experimental import pallas as pl
from jax.experimental.pallas import tpu as pltpu
from jax.sharding import PartitionSpec as P

VECS, ROWS, COLS = 8, 128, 256
TILES = ROWS // 8
WIDE = COLS + 128
TOP = 4
EXT = ROWS + 2 * TOP
REACH = 3
GROUP = 8
STRIP = 12
VMEM = pl.BlockSpec(memory_space=pltpu.VMEM)
SMEM = pl.BlockSpec(memory_space=pltpu.SMEM)


def lanes(rows):
    return lax.broadcasted_iota(jnp.int32, (rows, 128), 1)


def packed(tile_of, offset, turn):
    slot = lanes(8) // GROUP
    out = jnp.zeros((8, 128), jnp.float32)
    for t in range(TILES):
        target = (t + turn) % TILES
        moved = pltpu.roll(tile_of(t), (GROUP * target - offset) % 128, 1)
        out = jnp.where(slot == target, moved, out)
    return out


def edges_kernel(v_ref, onsite_ref, mask_ref, left_ref, right_ref, up_ref, down_ref):
    def present(rows, cols):
        return mask_ref[rows, cols].astype(jnp.float32)

    def vector(a, carry):
        def tile(t, cols):
            rows = pl.ds(8 * t, 8)
            return v_ref[a, rows, cols] * present(rows, cols)

        left_ref[a] = packed(lambda t: tile(t, pl.ds(0, 128)), 0, TILES // 2)
        right_ref[a] = packed(lambda t: tile(t, pl.ds(COLS - 128, 128)), 120, 0)
        return carry

    lax.fori_loop(0, VECS, vector, 0)

    def second(t, cols):
        return 0.25 * present(pl.ds(8 * t, 8), cols)

    def first(t, cols):
        return second(t, cols) * onsite_ref[pl.ds(8 * t, 8), cols]

    for k, coef in enumerate((first, second)):
        left_ref[VECS + k] = packed(lambda t: coef(t, pl.ds(0, 128)), 0, TILES // 2)
        right_ref[VECS + k] = packed(lambda t: coef(t, pl.ds(COLS - 128, 128)), 120, 0)
    for ref, t, start in ((up_ref, 0, 0), (down_ref, TILES - 1, 8 - REACH)):
        rows = pl.ds(8 * t, 8)
        block = v_ref[:, rows, :] * present(rows, slice(None))[None]
        block = jnp.swapaxes(block, 0, 1)
        for i in range(REACH):
            for h in range(2):
                ref[2 * i + h] = block[start + i, :, 128 * h : 128 * h + 128]
        for k, coef in enumerate((first, second)):
            for h in range(2):
                ref[2 * REACH + 2 * k + h] = coef(t, pl.ds(128 * h, 128))


def joined(from_left, from_right, left_slot, right_slot):
    lane = lanes(8)
    moved_left = pltpu.roll(from_left, (120 - GROUP * left_slot) % 128, 1)
    moved_right = pltpu.roll(from_right, (-GROUP * right_slot) % 128, 1)
    zero = jnp.zeros((8, 128), jnp.float32)
    return jnp.where(lane >= 120, moved_left, jnp.where(lane < GROUP, moved_right, zero))


def filter_kernel(c_ref, v0_ref, v1_ref, onsite_ref, mask_ref, vec_ref, coef_ref, out_ref, a_ref, b_ref, g_ref, d_ref, q_ref):
    half = TILES // 2
    main = slice(0, COLS)
    side = slice(COLS, WIDE)
    flats = [ref.reshape(VECS * ROWS, 128) for ref in (v0_ref, v1_ref)]

    def fill(t, carry):
        rows = pl.ds(pl.multiple_of(8 * t, 8), 8)
        second = mask_ref[rows, :].astype(jnp.float32)
        first = 0.25 * onsite_ref[rows, :]
        for i in range(8):
            present = jnp.broadcast_to(second[i : i + 1], (8, COLS))
            for h, flat in enumerate(flats):
                row = flat[pl.ds(8 * t + i, VECS, stride=ROWS), :]
                a_ref[TOP + 8 * t + i, :, 128 * h : 128 * h + 128] = row * present[:, 128 * h : 128 * h + 128]
            d_ref[TOP + 8 * t + i, :, main] = jnp.broadcast_to(first[i : i + 1], (8, COLS)) * present
            q_ref[TOP + 8 * t + i, :, main] = 0.25 * present
        return carry

    lax.fori_loop(0, TILES, fill, 0)
    west = jnp.swapaxes(vec_ref[0:8], 0, 1)
    east = jnp.swapaxes(vec_ref[8:16], 0, 1)
    for t in range(TILES):
        for i in range(8):
            a_ref[TOP + 8 * t + i, :, side] = joined(west[i], east[i], t, (t + half) % TILES)
        for k, ref in enumerate((d_ref, q_ref)):
            block = joined(coef_ref[k], coef_ref[2 + k], t, (t + half) % TILES)
            for i in range(8):
                ref[TOP + 8 * t + i, :, side] = jnp.broadcast_to(block[i : i + 1], (8, 128))
    for base, t, start, goal in ((0, TILES - 1, 8 - REACH, TOP - REACH), (1, 0, 0, TOP + ROWS)):
        at = 16 + base * (2 * REACH + 8)
        corner = jnp.swapaxes(vec_ref[at + 2 * REACH : at + 2 * REACH + 8], 0, 1)
        for i in range(REACH):
            for h in range(2):
                a_ref[goal + i, :, 128 * h : 128 * h + 128] = vec_ref[at + 2 * i + h]
            mixed = corner[start + i]
            a_ref[goal + i, :, side] = joined(mixed, mixed, t, (t + half) % TILES)
        at = 4 + base * 6
        for k, ref in enumerate((d_ref, q_ref)):
            mixed = coef_ref[at + 4 + k]
            block = joined(mixed, mixed, t, (t + half) % TILES)
            for i in range(REACH):
                for h in range(2):
                    row = coef_ref[at + 2 * k + h][start + i : start + i + 1]
                    ref[goal + i, :, 128 * h : 128 * h + 128] = jnp.broadcast_to(row, (8, 128))
                ref[goal + i, :, side] = jnp.broadcast_to(block[start + i : start + i + 1], (8, 128))
    for e in (TOP - REACH, TOP + ROWS + REACH - 1):
        b_ref[e] = jnp.zeros((VECS, WIDE), jnp.float32)
        g_ref[e] = jnp.zeros((VECS, WIDE), jnp.float32)

    even_lane = lax.broadcasted_iota(jnp.int32, (VECS, WIDE), 1) % 2 == 0

    def sweep(source, others, combine, start, count, strip=STRIP):
        def body(p, carry):
            e = start + strip * p
            rows = [source[e - 1 + k] for k in range(strip + 2)]
            coefs = [(d_ref[e + k], q_ref[e + k]) for k in range(strip)]
            loaded = [[ref[e + k] for ref in others] for k in range(strip)]
            stores = []
            for k in range(strip):
                above, centre, below = rows[k : k + 3]
                first, second = (below, above) if k % 2 == 0 else (above, below)
                near = pltpu.roll(centre, 1, 1) + pltpu.roll(centre, WIDE - 1, 1)
                near = near + jnp.where(even_lane, first, second)
                applied = coefs[k][0] * centre - coefs[k][1] * near
                stores.append((applied, centre, loaded[k]))
            combine(e, stores)
            return carry

        lax.fori_loop(0, count // strip, body, 0)

    def into(target, value):
        def combine(e, rows):
            for k, row in enumerate(rows):
                target[e + k] = value(*row)

        return combine

    c0, c1, c2, c3, c4 = (c_ref[k] for k in range(5))
    wide = ROWS + 4
    sweep(a_ref, (), into(b_ref, lambda s, x, o: c3 * x + (c4 + c4) * s), 2, wide)
    sweep(b_ref, (a_ref,), into(g_ref, lambda s, x, o: (c2 - c4) * o[0] + (s + s)), 2, wide)
    sweep(g_ref, (a_ref, b_ref), into(b_ref, lambda s, x, o: c1 * o[0] + ((s + s) - o[1])), 2, wide)
    sweep(b_ref, (a_ref, g_ref), into(g_ref, lambda s, x, o: c0 * o[0] + (s - o[1])), 2, wide)

    def finish(e, rows):
        for k, (applied, centre, _) in enumerate(rows):
            out_ref[e - TOP + k, 0:VECS, :] = centre[:, main]
            out_ref[e - TOP + k, VECS : 2 * VECS, :] = applied[:, main]

    sweep(g_ref, (), finish, TOP, ROWS, 8)


def parts_kernel(s0_ref, s1_ref, out_ref):
    count, rows, _ = s0_ref.shape
    for h, ref in enumerate((s0_ref, s1_ref)):
        flat = ref.reshape(count * rows, 128)
        cols = slice(128 * h, 128 * h + 128)
        for i in range(rows):
            block = flat[pl.ds(i, count, stride=rows), :]
            high = block.astype(jnp.bfloat16)
            out_ref[rows * pl.program_id(0) + i, 0:count, cols] = high
            out_ref[rows * pl.program_id(0) + i, count : 2 * count, cols] = (block - high.astype(jnp.float32)).astype(jnp.bfloat16)


def gram_kernel(x_ref, y_ref, s_ref, out_ref):
    def group(t, carry):
        total = None
        for k in range(16):
            r = 16 * t + k
            block = jnp.concatenate([x_ref[r], y_ref[r]], 0)
            high = block.astype(jnp.bfloat16)
            low = (block - high.astype(jnp.float32)).astype(jnp.bfloat16)
            product = lax.dot_general(
                jnp.concatenate([high, low], 0),
                s_ref[r],
                (((1,), (1,)), ((), ())),
                preferred_element_type=jnp.float32,
            )
            total = product if total is None else total + product
        return carry + total

    whole = lax.fori_loop(0, ROWS // 16, group, jnp.zeros((64, 128), jnp.float32))
    rows = whole[0:32, :] + whole[32:64, :]
    out_ref[...] = rows[:, 0:64] + rows[:, 64:128]


def floats(*shape):
    return jax.ShapeDtypeStruct(shape, jnp.float32)


def edges(block_vectors, onsite, mask):
    return pl.pallas_call(
        edges_kernel,
        name="edges",
        out_shape=tuple(floats(10, 8, 128) for _ in range(4)),
        in_specs=[VMEM] * 3,
        out_specs=(VMEM,) * 4,
        compiler_params=limit(4),
    )(block_vectors, onsite, mask)


def filtering(coefs, vectors, onsite, mask, vec_strips, coef_strips):
    return pl.pallas_call(
        filter_kernel,
        name="filtering",
        grid=(1,),
        out_shape=floats(ROWS, 2 * VECS, COLS),
        in_specs=[
            SMEM,
            pl.BlockSpec((VECS, ROWS, 128), lambda t: (0, 0, 0)),
            pl.BlockSpec((VECS, ROWS, 128), lambda t: (0, 0, 1)),
        ] + [VMEM] * 4,
        out_specs=VMEM,
        scratch_shapes=[pltpu.VMEM((EXT, VECS, WIDE), jnp.float32)] * 5,
        compiler_params=limit(18),
    )(coefs, vectors, vectors, onsite, mask, vec_strips, coef_strips)


def parts(search):
    count = search.shape[0]
    return pl.pallas_call(
        parts_kernel,
        name="parts",
        grid=(TILES,),
        out_shape=jax.ShapeDtypeStruct((ROWS, 2 * count, COLS), jnp.bfloat16),
        in_specs=[
            pl.BlockSpec((count, 8, 128), lambda t: (0, t, 0)),
            pl.BlockSpec((count, 8, 128), lambda t: (0, t, 1)),
        ],
        out_specs=VMEM,
        compiler_params=limit(12),
    )(search, search)


def gram(x, y, split):
    return pl.pallas_call(
        gram_kernel,
        name="gram",
        out_shape=floats(32, 64),
        in_specs=[VMEM] * 3,
        out_specs=VMEM,
        compiler_params=limit(20),
    )(x, y, split)


def limit(mib):
    return pltpu.CompilerParams(vmem_limit_bytes=mib << 20)


def shifted(block, axis, by):
    count = lax.axis_size(axis)
    return lax.ppermute(block, axis, [(i, i + by) for i in range(count) if 0 <= i + by < count])


def copies_sum(partial, axis):
    count = lax.axis_size(axis)
    copies = jnp.broadcast_to(partial[None], (count,) + partial.shape)
    return lax.all_to_all(copies, axis, 0, 0).sum(0)


def shards(block_vectors, search_vectors, onsite_energy, site_mask, filter_coefs):
    across = [(0, 2), (1, 3), (2, 0), (3, 1)]
    swap = [(0, 1), (1, 0), (2, 3), (3, 2)]
    left, right, up, down = edges(block_vectors, onsite_energy, site_mask)
    from_left = shifted(right, "ly", 1)
    from_right = shifted(left, "ly", -1)
    from_left, from_right, block_vectors, search_vectors = lax.optimization_barrier(
        (from_left, from_right, block_vectors, search_vectors)
    )
    far_vectors = lax.ppermute(block_vectors, "blk", across)
    slot = lax.broadcasted_iota(jnp.int32, (10, 8, 128), 2) // GROUP
    from_below = shifted(jnp.concatenate([up, jnp.where(slot == 0, from_left, from_right)], 0), "lx", -1)
    from_above = shifted(jnp.concatenate([down, jnp.where(slot == TILES - 1, from_left, from_right)], 0), "lx", 1)
    vec_strips = jnp.concatenate(
        [from_left[:8], from_right[:8]]
        + [x for f in (from_above, from_below) for x in (f[:6], f[10:18])], 0
    )
    coef_strips = jnp.concatenate(
        [from_left[8:], from_right[8:]]
        + [x for f in (from_above, from_below) for x in (f[6:10], f[18:])], 0
    )
    far_strips = lax.ppermute(vec_strips, "blk", across)
    split = parts(search_vectors)
    split, own_strips = lax.optimization_barrier((split, vec_strips))
    own = filtering(filter_coefs, block_vectors, onsite_energy, site_mask, own_strips, coef_strips)
    own_near = lax.ppermute(own, "blk", swap)
    far = filtering(filter_coefs, far_vectors, onsite_energy, site_mask, far_strips, coef_strips)
    far_near = lax.ppermute(far, "blk", swap)
    partial = jnp.concatenate([gram(own, own_near, split), gram(far, far_near, split)], 0)
    total = copies_sum(copies_sum(partial.reshape(32, 128), "ly"), "lx").reshape(4, 2, VECS, 64)
    block = lax.axis_index("blk")
    total = jnp.where(block % 2 == 1, total[jnp.array([1, 0, 3, 2])], total)
    total = jnp.where(block >= 2, total[jnp.array([2, 3, 0, 1])], total)
    nrows, ncols = onsite_energy.shape
    scale = 1.0 / math.sqrt(nrows * ncols * lax.axis_size("lx") * lax.axis_size("ly"))
    return jnp.swapaxes(total, 0, 1).reshape(2, 4 * VECS, 64) * scale


def solution(mesh):
    placed = (P("blk", "lx", "ly"), P("blk", "lx", "ly"), P("lx", "ly"), P("lx", "ly"), P())
    return jax.shard_map(
        shards, mesh=mesh, in_specs=placed, out_specs=P(None, None, "blk"), check_vma=False
    )
```

time: 538 us -> 107 us (0.20)
  blocking collectives: 310 us -> 12.3 us
  waiting for transfers between devices: 90.3 us -> 28.1 us
  starting transfers between devices: 62.9 us -> 23.6 us
  Pallas kernels: 0 us -> 33.2 us
  other arithmetic: 22.4 us -> 0.71 us
  matrix products: 16.7 us -> 0 us
  between operations: 14.3 us -> 0.28 us
  local copies, waits for them, and re-layouts: 20.9 us -> 8.41 us
    psum x1 -> x0, blocking collectives: 310 us -> none  [shards(): total = lax.psum(partial_gram, ('lx', 'ly'))]
    all_gather x1 -> x0, waiting for transfers between devices: 71.7 us -> none  [shards(): lax.all_gather(paired, 'blk', axis=1, tiled=True)]
    ppermute x20 -> x8, starting transfers between devices: 62.9 us -> 13.5 us  [the longest x4 9.6 us: shifted(): lax.ppermute(block, axis, [(i, i + by) for i in range(count) if 0 <= i +...]
    pallas_call x0 -> x6, Pallas kernels: none -> 33.2 us  [the longest x2 20.8 us: filtering(): pl.pallas_call(filter_kernel, name='filtering', grid=(1,), out_shape=floa...]
    dot_general x1 -> x0, matrix products: 16.7 us -> none  [gram_rows(): lax.dot_general(flat, search_flat, (((1,), (1,)), ((), ())), precision=la...]
    all_to_all x0 -> x1, blocking collectives: none -> 12.3 us  [copies_sum(): return lax.all_to_all(copies, axis, 0, 0).sum(0)]
    slice x21 -> x0, local copies, waits for them, and re-layouts: 10.7 us -> none  [the longest x10 8.27 us: extended(): lax.slice_in_dim(block, block.shape[dim] - width, None, axis=dim)]
    ppermute x10 -> x0, local copies, waits for them, and re-layouts: 10.2 us -> none  [the longest x5 5.86 us: extended(): lax.ppermute(lax.slice_in_dim(block, 0, width, axis=dim), axis, backward)]
  transfers between devices with their start and end apart: 21 -> 9, of which waited for: 11 -> 5; matrix products, arithmetic and copies ran while one was open for 1% -> 0% of each run, Pallas kernels for 0% -> 27%
where the time goes in v2:
time: 107 us
  Pallas kernels  33.2 us (31%)
  waiting for transfers between devices  28.1 us (26%)
  starting transfers between devices  23.6 us (22%)
  blocking collectives  12.3 us (11%)
  local copies, waits for them, and re-layouts  8.41 us (8%)
    pallas_call x2, Pallas kernels, filtering(): pl.pallas_call(filter_kernel, name='filtering', grid=(1,), out_shape=floa...  20.8 us
    ppermute x1, waiting for transfers between devices, shards(): far_strips = lax.ppermute(vec_strips, 'blk', across)  14.3 us
    all_to_all x1, blocking collectives, copies_sum(): return lax.all_to_all(copies, axis, 0, 0).sum(0)  12.3 us
    all_to_all x1, starting transfers between devices, copies_sum(): return lax.all_to_all(copies, axis, 0, 0).sum(0)  10.1 us
    ppermute x4, starting transfers between devices, shifted(): lax.ppermute(block, axis, [(i, i + by) for i in range(count) if 0 <= i +...  9.6 us
    all_to_all x1, waiting for transfers between devices, copies_sum(): return lax.all_to_all(copies, axis, 0, 0).sum(0)  9.05 us
    pallas_call x2, Pallas kernels, gram(): pl.pallas_call(gram_kernel, name='gram', out_shape=floats(32, 64), in_spe...  7.89 us
    unnamed x30, local copies, waits for them, and re-layouts  6.46 us
  transfers between devices with their start and end apart: 9, of which 5 were waited for; matrix products, arithmetic and copies ran while one was open for 0% of the time, Pallas kernels for 27%

profile of v2, /device:TPU:16, one launch (start us, length us, event | category | flops | bytes accessed | tf_op | source)
XLA Modules:
  0.0 106.6 jit_solution(1548953276576181972)
XLA Ops:
  0.0 1.2 %copy-done.1 = f32[8,128,256]{2,1,0:T(8,128)S(1)} copy-done((f32[8,128,256]{2,1,0:T(8,128)S(1)}, f32[8,128,256]{2,1,0:T(8,128)}, u32[]{:S(2)}) %copy-start.1) | copy-done | bytes 1048600
  1.2 0.9 copy-done.3
  2.1 0.9 copy-done.5
  3.0 0.9 edges.1
  4.0 3.2 %collective-permute-start = (f32[10,8,128]{2,1,0:T(8,128)S(1)}, f32[10,8,128]{2,1,0:T(8,128)S(1)}, u32[]{:S(2)}, u32[]{:S(2)}) collective-permute-start(f32[10,8,128]{2,1,0:T(8,128)S(1)} %get-tuple-element.15), channel_id=1, source_target_pairs={{0,4},{4,8},{8,12},{12,16},{16,20},{20,24},{24,28},{1,5},{5,9},{9,... | collective-permute-start | bytes 122888 | tf_op jit(solution)/shard_map/ppermute | solution.py:272
  7.2 1.3 %collective-permute-start.1 = (f32[10,8,128]{2,1,0:T(8,128)S(1)}, f32[10,8,128]{2,1,0:T(8,128)S(1)}, u32[]{:S(2)}, u32[]{:S(2)}) collective-permute-start(f32[10,8,128]{2,1,0:T(8,128)S(1)} %get-tuple-element.16), channel_id=1, source_target_pairs={{4,0},{8,4},{12,8},{16,12},{20,16},{24,20},{28,24},{5,1},{9,5},{13... | collective-permute-start | bytes 122888 | tf_op jit(solution)/shard_map/ppermute | solution.py:272
  8.8 4.2 %collective-permute-done.1 = f32[10,8,128]{2,1,0:T(8,128)S(1)} collective-permute-done((f32[10,8,128]{2,1,0:T(8,128)S(1)}, f32[10,8,128]{2,1,0:T(8,128)S(1)}, u32[]{:S(2)}, u32[]{:S(2)}) %collective-permute-start.1) | collective-permute-done | bytes 40992 | tf_op jit(solution)/shard_map/ppermute | solution.py:272
  13.1 3.8 %collective-permute-start.2 = (f32[20,8,128]{2,1,0:T(8,128)S(1)}, f32[20,8,128]{2,1,0:T(8,128)S(1)}, u32[]{:S(2)}, u32[]{:S(2)}) collective-permute-start(f32[20,8,128]{2,1,0:T(8,128)S(1)} %pad_maximum_fusion), channel_id=1, source_target_pairs={{0,32},{32,64},{64,96},{96,128},{128,160},{160,192},{192,224},{1,3... | collective-permute-start | bytes 245768 | tf_op jit(solution)/shard_map/ppermute | solution.py:272
  17.0 1.3 %collective-permute-start.3 = (f32[20,8,128]{2,1,0:T(8,128)S(1)}, f32[20,8,128]{2,1,0:T(8,128)S(1)}, u32[]{:S(2)}, u32[]{:S(2)}) collective-permute-start(f32[20,8,128]{2,1,0:T(8,128)S(1)} %pad_maximum_fusion.1), channel_id=1, source_target_pairs={{32,0},{64,32},{96,64},{128,96},{160,128},{192,160},{224,192},{33,... | collective-permute-start | bytes 245768 | tf_op jit(solution)/shard_map/ppermute | solution.py:272
  18.3 3.4 %copy-done = f32[64,128,256]{2,1,0:T(8,128)S(1)} copy-done((f32[64,128,256]{2,1,0:T(8,128)S(1)}, f32[64,128,256]{2,1,0:T(8,128)}, u32[]{:S(2)}) %copy-start) | copy-done | bytes 8388632
  21.7 3.5 %parts.1.s_ref = bf16[128,128,256]{2,1,0:T(8,128)(2,1)S(1)} custom-call(f32[64,128,256]{2,1,0:T(8,128)S(1)} %copy-done, f32[64,128,256]{2,1,0:T(8,128)S(1)} %copy-done), custom_call_target="tpu_custom_call" | custom-call | tf_op jit(solution)/shard_map/parts/pallas_call | solution.py:241
  25.2 0.7 collective-permute-start.5
  26.0 3.0 %collective-permute-start.6 = (f32[44,8,128]{2,1,0:T(8,128)S(1)}, f32[44,8,128]{2,1,0:T(8,128)S(1)}, u32[]{:S(2)}, u32[]{:S(2)}) collective-permute-start(f32[44,8,128]{2,1,0:T(8,128)S(1)} %slice_dynamic-update-slice_fusion.vec_ref), channel_id=1, source_target_pairs={{0,2},{1,3},{2,0},{3,1},{4,6},{5,7},{6,4},{7,5},{8,10},{9,11},{10,... | collective-permute-start | bytes 540680 | tf_op jit(solution)/shard_map/ppermute | solution.py:302
  29.0 10.4 %filtering.2.x_ref = f32[128,16,256]{2,1,0:T(8,128)S(1)} custom-call(f32[5]{0:T(128)S(1)} %copy-done.7, f32[8,128,256]{2,1,0:T(8,128)S(1)} %copy-done.2, f32[8,128,256]{2,1,0:T(8,128)S(1)} %copy-done.2, f32[128,256]{1,0:T(8,128)S(1)} %copy-done.4, s32[128,256]{1,0:T(8,128)S(1)} %copy-done.6, f32[44,8,128]{2,1,0:T(8,128)S(1)} %slice_dynamic-update-slice_fusion.vec_ref, ...), custom_call_target="tpu_custom_call" | custom-call | tf_op jit(solution)/shard_map/filtering/pallas_call | solution.py:223
  39.5 14.3 %collective-permute-done.6.vec_ref = f32[44,8,128]{2,1,0:T(8,128)S(1)} collective-permute-done((f32[44,8,128]{2,1,0:T(8,128)S(1)}, f32[44,8,128]{2,1,0:T(8,128)S(1)}, u32[]{:S(2)}, u32[]{:S(2)}) %collective-permute-start.6) | collective-permute-done | bytes 180256 | tf_op jit(solution)/shard_map/ppermute | solution.py:302
  53.9 10.4 %filtering.3.x_ref = f32[128,16,256]{2,1,0:T(8,128)S(1)} custom-call(f32[5]{0:T(128)S(1)} %copy-done.7, f32[8,128,256]{2,1,0:T(8,128)S(1)} %collective-permute-done.5.v0_ref.v1_ref, f32[8,128,256]{2,1,0:T(8,128)S(1)} %collective-permute-done.5.v0_ref.v1_ref, f32[128,256]{1,0:T(8,128)S(1)} %copy-done.4, s32[128,256]{1,0:T(8,128)S(1)} %copy-done.6, ...), custom_call_target="tpu_custom_call" | custom-call | tf_op jit(solution)/shard_map/filtering/pallas_call | solution.py:223
  64.4 3.9 %gram.2 = f32[32,64]{1,0:T(8,128)S(1)} custom-call(f32[128,16,256]{2,1,0:T(8,128)S(1)} %filtering.2.x_ref, f32[128,16,256]{2,1,0:T(8,128)S(1)} %collective-permute-done.4.y_ref, bf16[128,128,256]{2,1,0:T(8,128)(2,1)S(1)} %parts.1.s_ref), custom_call_target="tpu_custom_call" | custom-call | tf_op jit(solution)/shard_map/gram/pallas_call | solution.py:256
  68.5 3.9 %gram.3 = f32[32,64]{1,0:T(8,128)S(1)} custom-call(f32[128,16,256]{2,1,0:T(8,128)S(1)} %filtering.3.x_ref, f32[128,16,256]{2,1,0:T(8,128)S(1)} %collective-permute-done.7.y_ref, bf16[128,128,256]{2,1,0:T(8,128)(2,1)S(1)} %parts.1.s_ref), custom_call_target="tpu_custom_call" | custom-call | tf_op jit(solution)/shard_map/gram/pallas_call | solution.py:256
  72.6 12.3 %all_to_all.10 = f32[8,32,128]{2,1,0:T(8,128)S(1)} all-to-all(f32[8,32,128]{2,1,0:T(8,128)S(1)} %broadcast_in_dim.20), channel_id=1, replica_groups=mesh['lx'=8,'ly'=8,'blk'=4] {'ly'}, dimensions={0} | all-to-all | bytes 262144 | tf_op jit(solution)/shard_map/all_to_all | solution.py:278
  84.9 0.7 broadcast_in_dim.21
  85.6 10.1 %all-to-all-start.1 = ((f32[8,32,128]{2,1,0:T(8,128)}), f32[8,32,128]{2,1,0:T(8,128)S(1)}, u32[]{:S(2)}, u32[]{:S(2)}) async-start(f32[8,32,128]{2,1,0:T(8,128)} %broadcast_in_dim.21), calls=%async_computation.1 | async-start | bytes 262144 | tf_op jit(solution)/shard_map/all_to_all | solution.py:278
  95.7 9.0 %all-to-all-done.1 = f32[8,32,128]{2,1,0:T(8,128)S(1)} async-done(((f32[8,32,128]{2,1,0:T(8,128)}), f32[8,32,128]{2,1,0:T(8,128)S(1)}, u32[]{:S(2)}, u32[]{:S(2)}) %all-to-all-start.1) | async-done | bytes 131104 | tf_op jit(solution)/shard_map/all_to_all | solution.py:278
  105.4 0.6 gather_fusion.1
  106.0 0.6 copy_bitcast_fusion
  (50 shorter events, 1.6 us)
Async XLA Ops:
  0.0 1.2 %copy-start.1 = (f32[8,128,256]{2,1,0:T(8,128)S(1)}, f32[8,128,256]{2,1,0:T(8,128)}, u32[]{:S(2)}) copy-start(f32[8,128,256]{2,1,0:T(8,128)} %v1_ref) | copy-start | bytes 3145732
  1.2 0.9 copy-start.3
  2.1 0.9 copy-start.5
  4.0 4.9 %collective-permute-start = (f32[10,8,128]{2,1,0:T(8,128)S(1)}, f32[10,8,128]{2,1,0:T(8,128)S(1)}, u32[]{:S(2)}, u32[]{:S(2)}) collective-permute-start(f32[10,8,128]{2,1,0:T(8,128)S(1)} %get-tuple-element.15), channel_id=1, source_target_pairs={{0,4},{4,8},{8,12},{12,16},{16,20},{20,24},{24,28},{1,5},{5,9},{9,... | collective-permute-start | bytes 122888 | tf_op jit(solution)/shard_map/ppermute | solution.py:272
  7.2 5.9 %collective-permute-start.1 = (f32[10,8,128]{2,1,0:T(8,128)S(1)}, f32[10,8,128]{2,1,0:T(8,128)S(1)}, u32[]{:S(2)}, u32[]{:S(2)}) collective-permute-start(f32[10,8,128]{2,1,0:T(8,128)S(1)} %get-tuple-element.16), channel_id=1, source_target_pairs={{4,0},{8,4},{12,8},{16,12},{20,16},{24,20},{28,24},{5,1},{9,5},{13... | collective-permute-start | bytes 122888 | tf_op jit(solution)/shard_map/ppermute | solution.py:272
  13.1 12.9 %collective-permute-start.2 = (f32[20,8,128]{2,1,0:T(8,128)S(1)}, f32[20,8,128]{2,1,0:T(8,128)S(1)}, u32[]{:S(2)}, u32[]{:S(2)}) collective-permute-start(f32[20,8,128]{2,1,0:T(8,128)S(1)} %pad_maximum_fusion), channel_id=1, source_target_pairs={{0,32},{32,64},{64,96},{96,128},{128,160},{160,192},{192,224},{1,3... | collective-permute-start | bytes 245768 | tf_op jit(solution)/shard_map/ppermute | solution.py:272
  17.0 9.0 %collective-permute-start.3 = (f32[20,8,128]{2,1,0:T(8,128)S(1)}, f32[20,8,128]{2,1,0:T(8,128)S(1)}, u32[]{:S(2)}, u32[]{:S(2)}) collective-permute-start(f32[20,8,128]{2,1,0:T(8,128)S(1)} %pad_maximum_fusion.1), channel_id=1, source_target_pairs={{32,0},{64,32},{96,64},{128,96},{160,128},{192,160},{224,192},{33,... | collective-permute-start | bytes 245768 | tf_op jit(solution)/shard_map/ppermute | solution.py:272
  18.3 3.4 %copy-start = (f32[64,128,256]{2,1,0:T(8,128)S(1)}, f32[64,128,256]{2,1,0:T(8,128)}, u32[]{:S(2)}) copy-start(f32[64,128,256]{2,1,0:T(8,128)} %s1_ref) | copy-start | bytes 25165828
  21.7 3.6 %copy-start.2 = (f32[8,128,256]{2,1,0:T(8,128)S(1)}, f32[8,128,256]{2,1,0:T(8,128)}, u32[]{:S(2)}) copy-start(f32[8,128,256]{2,1,0:T(8,128)} %v1_ref) | copy-start | bytes 3145732
  21.7 7.3 %copy-start.4 = (f32[128,256]{1,0:T(8,128)S(1)}, f32[128,256]{1,0:T(8,128)}, u32[]{:S(2)}) copy-start(f32[128,256]{1,0:T(8,128)} %onsite_ref.5) | copy-start | bytes 393220
  21.7 7.4 %copy-start.6 = (s32[128,256]{1,0:T(8,128)S(1)}, s32[128,256]{1,0:T(8,128)}, u32[]{:S(2)}) copy-start(s32[128,256]{1,0:T(8,128)} %mask_ref.5) | copy-start | bytes 393220
  21.7 7.4 %copy-start.7 = (f32[5]{0:T(128)S(1)}, f32[5]{0:T(128)}, u32[]{:S(2)}) copy-start(f32[5]{0:T(128)} %c_ref.3) | copy-start | bytes 64
  25.2 28.6 %collective-permute-start.5 = (f32[8,128,256]{2,1,0:T(8,128)S(1)}, f32[8,128,256]{2,1,0:T(8,128)S(1)}, u32[]{:S(2)}, u32[]{:S(2)}) collective-permute-start(f32[8,128,256]{2,1,0:T(8,128)S(1)} %copy-done.2), channel_id=1, source_target_pairs={{0,2},{1,3},{2,0},{3,1},{4,6},{5,7},{6,4},{7,5},{8,10},{9,11},{10,... | collective-permute-start | bytes 3145736 | tf_op jit(solution)/shard_map/ppermute | solution.py:290
  26.0 27.9 %collective-permute-start.6 = (f32[44,8,128]{2,1,0:T(8,128)S(1)}, f32[44,8,128]{2,1,0:T(8,128)S(1)}, u32[]{:S(2)}, u32[]{:S(2)}) collective-permute-start(f32[44,8,128]{2,1,0:T(8,128)S(1)} %slice_dynamic-update-slice_fusion.vec_ref), channel_id=1, source_target_pairs={{0,2},{1,3},{2,0},{3,1},{4,6},{5,7},{6,4},{7,5},{8,10},{9,11},{10,... | collective-permute-start | bytes 540680 | tf_op jit(solution)/shard_map/ppermute | solution.py:302
  39.4 25.0 %collective-permute-start.4 = (f32[128,16,256]{2,1,0:T(8,128)S(1)}, f32[128,16,256]{2,1,0:T(8,128)S(1)}, u32[]{:S(2)}, u32[]{:S(2)}) collective-permute-start(f32[128,16,256]{2,1,0:T(8,128)S(1)} %filtering.2.x_ref), channel_id=1, source_target_pairs={{0,1},{1,0},{2,3},{3,2},{4,5},{5,4},{6,7},{7,6},{8,9},{9,8},{10,11... | collective-permute-start | bytes 6291464 | tf_op jit(solution)/shard_map/ppermute | solution.py:306
  64.3 4.2 %collective-permute-start.7 = (f32[128,16,256]{2,1,0:T(8,128)S(1)}, f32[128,16,256]{2,1,0:T(8,128)S(1)}, u32[]{:S(2)}, u32[]{:S(2)}) collective-permute-start(f32[128,16,256]{2,1,0:T(8,128)S(1)} %filtering.3.x_ref), channel_id=1, source_target_pairs={{0,1},{1,0},{2,3},{3,2},{4,5},{5,4},{6,7},{7,6},{8,9},{9,8},{10,11... | collective-permute-start | bytes 6291464 | tf_op jit(solution)/shard_map/ppermute | solution.py:308
  68.3 27.3 %copy-start.8 = (s32[4]{0:T(128)S(1)}, s32[4]{0:T(128)}, u32[]{:S(2)}) copy-start(s32[4]{0:T(128)} %constant.60) | copy-start | bytes 52
  68.4 27.3 %copy-start.9 = (s32[4]{0:T(128)S(1)}, s32[4]{0:T(128)}, u32[]{:S(2)}) copy-start(s32[4]{0:T(128)} %constant.61) | copy-start | bytes 52
  85.6 19.2 %all-to-all-start.1 = ((f32[8,32,128]{2,1,0:T(8,128)}), f32[8,32,128]{2,1,0:T(8,128)S(1)}, u32[]{:S(2)}, u32[]{:S(2)}) async-start(f32[8,32,128]{2,1,0:T(8,128)} %broadcast_in_dim.21), calls=%async_computation.1 | async-start | bytes 262144 | tf_op jit(solution)/shard_map/all_to_all | solution.py:278

commit v3 on v2

v3 whole, which is shorter than its diff:
```python
import functools
import math

import jax
import jax.numpy as jnp
from jax import lax
from jax.experimental import pallas as pl
from jax.experimental.pallas import tpu as pltpu
from jax.sharding import PartitionSpec as P


VECS, ROWS, COLS = 8, 128, 256
TILES = ROWS // 8
WIDE = COLS + 128
TOP = 4
EXT = ROWS + 2 * TOP
REACH = 3
GROUP = 8
STRIP = 22
VMEM = pl.BlockSpec(memory_space=pltpu.VMEM)
HBM = pl.BlockSpec(memory_space=pltpu.HBM)
SMEM = pl.BlockSpec(memory_space=pltpu.SMEM)


def lanes(rows):
    return lax.broadcasted_iota(jnp.int32, (rows, 128), 1)


def packed(tile_of, offset, turn):
    slot = lanes(8) // GROUP
    out = jnp.zeros((8, 128), jnp.float32)
    for t in range(TILES):
        target = (t + turn) % TILES
        moved = pltpu.roll(tile_of(t), (GROUP * target - offset) % 128, 1)
        out = jnp.where(slot == target, moved, out)
    return out


def edges_kernel(
    v_hbm, onsite_hbm, mask_hbm, left_ref, right_ref, up_ref, down_ref, v_ref, onsite_ref, mask_ref, sems
):
    copies = [
        pltpu.make_async_copy(source, target, sems.at[k])
        for k, (source, target) in enumerate(
            ((v_hbm, v_ref), (onsite_hbm, onsite_ref), (mask_hbm, mask_ref))
        )
    ]
    for copy in copies:
        copy.start()
    for copy in copies:
        copy.wait()

    def present(rows, cols):
        return mask_ref[rows, cols].astype(jnp.float32)

    def vector(a, carry):
        def tile(t, cols):
            rows = pl.ds(8 * t, 8)
            return v_ref[a, rows, cols] * present(rows, cols)

        left_ref[a] = packed(lambda t: tile(t, pl.ds(0, 128)), 0, TILES // 2)
        right_ref[a] = packed(lambda t: tile(t, pl.ds(COLS - 128, 128)), 120, 0)
        return carry

    lax.fori_loop(0, VECS, vector, 0)

    def second(t, cols):
        return 0.5 * present(pl.ds(8 * t, 8), cols)

    def first(t, cols):
        return second(t, cols) * onsite_ref[pl.ds(8 * t, 8), cols]

    for k, coef in enumerate((first, second)):
        left_ref[VECS + k] = packed(lambda t: coef(t, pl.ds(0, 128)), 0, TILES // 2)
        right_ref[VECS + k] = packed(lambda t: coef(t, pl.ds(COLS - 128, 128)), 120, 0)
    for ref, t, start in ((up_ref, 0, 0), (down_ref, TILES - 1, 8 - REACH)):
        rows = pl.ds(8 * t, 8)
        block = v_ref[:, rows, :] * present(rows, slice(None))[None]
        block = jnp.swapaxes(block, 0, 1)
        for i in range(REACH):
            for h in range(2):
                ref[2 * i + h] = block[start + i, :, 128 * h : 128 * h + 128]
        for k, coef in enumerate((first, second)):
            for h in range(2):
                ref[2 * REACH + 2 * k + h] = coef(t, pl.ds(128 * h, 128))


def joined(from_left, from_right, left_slot, right_slot):
    lane = lanes(8)
    moved_left = pltpu.roll(from_left, (120 - GROUP * left_slot) % 128, 1)
    moved_right = pltpu.roll(from_right, (-GROUP * right_slot) % 128, 1)
    zero = jnp.zeros((8, 128), jnp.float32)
    return jnp.where(lane >= 120, moved_left, jnp.where(lane < GROUP, moved_right, zero))


def fill_vectors(v_refs, mask_ref, vec_ref, a_ref):
    half = TILES // 2
    side = slice(COLS, WIDE)
    flats = [ref.reshape(VECS * ROWS, 128) for ref in v_refs]

    def fill(t, carry):
        present = mask_ref[pl.ds(pl.multiple_of(8 * t, 8), 8), :].astype(jnp.float32)
        for i in range(8):
            for h, flat in enumerate(flats):
                row = flat[pl.ds(8 * t + i, VECS, stride=ROWS), :]
                kept = jnp.broadcast_to(present[i : i + 1, 128 * h : 128 * h + 128], (8, 128))
                a_ref[TOP + 8 * t + i, :, 128 * h : 128 * h + 128] = row * kept
        return carry

    lax.fori_loop(0, TILES, fill, 0)
    west = jnp.swapaxes(vec_ref[0:8], 0, 1)
    east = jnp.swapaxes(vec_ref[8:16], 0, 1)
    for t in range(TILES):
        for i in range(8):
            a_ref[TOP + 8 * t + i, :, side] = joined(west[i], east[i], t, (t + half) % TILES)
    for base, t, start, goal in ((0, TILES - 1, 8 - REACH, TOP - REACH), (1, 0, 0, TOP + ROWS)):
        at = 16 + base * (2 * REACH + 8)
        corner = jnp.swapaxes(vec_ref[at + 2 * REACH : at + 2 * REACH + 8], 0, 1)
        for i in range(REACH):
            for h in range(2):
                a_ref[goal + i, :, 128 * h : 128 * h + 128] = vec_ref[at + 2 * i + h]
            mixed = corner[start + i]
            a_ref[goal + i, :, side] = joined(mixed, mixed, t, (t + half) % TILES)


def fill_coefs(onsite_ref, mask_ref, coef_ref, d_ref, q_ref):
    half = TILES // 2
    main = slice(0, COLS)
    side = slice(COLS, WIDE)

    def fill(t, carry):
        rows = pl.ds(pl.multiple_of(8 * t, 8), 8)
        second = 0.5 * mask_ref[rows, :].astype(jnp.float32)
        first = second * onsite_ref[rows, :]
        for i in range(8):
            d_ref[TOP + 8 * t + i, :, main] = jnp.broadcast_to(first[i : i + 1], (8, COLS))
            q_ref[TOP + 8 * t + i, :, main] = jnp.broadcast_to(second[i : i + 1], (8, COLS))
        return carry

    lax.fori_loop(0, TILES, fill, 0)
    for t in range(TILES):
        for k, ref in enumerate((d_ref, q_ref)):
            block = joined(coef_ref[k], coef_ref[2 + k], t, (t + half) % TILES)
            for i in range(8):
                ref[TOP + 8 * t + i, :, side] = jnp.broadcast_to(block[i : i + 1], (8, 128))
    for base, t, start, goal in ((0, TILES - 1, 8 - REACH, TOP - REACH), (1, 0, 0, TOP + ROWS)):
        at = 4 + base * 6
        for k, ref in enumerate((d_ref, q_ref)):
            mixed = coef_ref[at + 4 + k]
            block = joined(mixed, mixed, t, (t + half) % TILES)
            for i in range(REACH):
                for h in range(2):
                    row = coef_ref[at + 2 * k + h][start + i : start + i + 1]
                    ref[goal + i, :, 128 * h : 128 * h + 128] = jnp.broadcast_to(row, (8, 128))
                ref[goal + i, :, side] = jnp.broadcast_to(block[start + i : start + i + 1], (8, 128))


def own_kernel(c_ref, v0_ref, v1_ref, onsite_ref, mask_ref, vec_ref, coef_ref, out_ref, d_ref, q_ref, *scratch):
    fill_coefs(onsite_ref, mask_ref, coef_ref, d_ref, q_ref)
    fill_vectors((v0_ref, v1_ref), mask_ref, vec_ref, scratch[0])
    sweeps(c_ref, d_ref, q_ref, out_ref, *scratch)


def far_kernel(c_ref, v0_ref, v1_ref, mask_ref, vec_ref, d_ref, q_ref, out_ref, *scratch):
    fill_vectors((v0_ref, v1_ref), mask_ref, vec_ref, scratch[0])
    sweeps(c_ref, d_ref, q_ref, out_ref, *scratch)


def sweeps(c_ref, d_ref, q_ref, out_ref, a_ref, b_ref, g_ref):
    main = slice(0, COLS)
    for e in (TOP - REACH, TOP + ROWS + REACH - 1):
        b_ref[e] = jnp.zeros((VECS, WIDE), jnp.float32)
        g_ref[e] = jnp.zeros((VECS, WIDE), jnp.float32)
    even_lane = lax.broadcasted_iota(jnp.int32, (VECS, WIDE), 1) % 2 == 0

    def sweep(source, others, combine, start, count, strip):
        def body(p, carry):
            e = start + strip * p
            rows = [source[e - 1 + k] for k in range(strip + 2)]
            coefs = [(d_ref[e + k], q_ref[e + k]) for k in range(strip)]
            loaded = [[ref[e + k] for ref in others] for k in range(strip)]
            stores = []
            for k in range(strip):
                above, centre, below = rows[k : k + 3]
                first, second = (below, above) if k % 2 == 0 else (above, below)
                near = pltpu.roll(centre, 1, 1) + pltpu.roll(centre, WIDE - 1, 1)
                near = near + jnp.where(even_lane, first, second)
                twice = coefs[k][0] * centre - coefs[k][1] * near
                stores.append((twice, centre, loaded[k]))
            combine(e, stores)
            return carry

        lax.fori_loop(0, count // strip, body, 0)

    def into(target, value):
        def combine(e, rows):
            for k, row in enumerate(rows):
                target[e + k] = value(*row)

        return combine

    c0, c1, c2, c3, c4 = (c_ref[k] for k in range(5))
    wide = ROWS + 4
    sweep(a_ref, (), into(b_ref, lambda s, x, o: c3 * x + c4 * s), 2, wide, STRIP)
    sweep(b_ref, (a_ref,), into(g_ref, lambda s, x, o: (c2 - c4) * o[0] + s), 2, wide, STRIP)
    sweep(g_ref, (a_ref, b_ref), into(b_ref, lambda s, x, o: c1 * o[0] + (s - o[1])), 2, wide, STRIP)
    sweep(b_ref, (a_ref, g_ref), into(g_ref, lambda s, x, o: c0 * o[0] + (0.5 * s - o[1])), 2, wide, STRIP)

    def finish(e, rows):
        for k, (twice, centre, _) in enumerate(rows):
            out_ref[e - TOP + k, 0:VECS, :] = centre[:, main]
            out_ref[e - TOP + k, VECS : 2 * VECS, :] = twice[:, main]

    sweep(g_ref, (), finish, TOP, ROWS, 16)


def parts_kernel(first, s_hbm, out_ref, buffer, sems):
    count = s_hbm.shape[0]
    rows = ROWS // 2
    copies = [
        pltpu.make_async_copy(
            s_hbm.at[:, pl.ds(first + 8 * t, 8), pl.ds(128 * h, 128)],
            buffer.at[h, :, pl.ds(8 * t, 8), :],
            sems.at[t, h],
        )
        for t in range(rows // 8)
        for h in range(2)
    ]
    for copy in copies:
        copy.start()
    flat = buffer.reshape(2 * count * rows, 128)
    for t in range(rows // 8):
        copies[2 * t].wait()
        copies[2 * t + 1].wait()

        def split(i, carry):
            for h in range(2):
                cols = slice(128 * h, 128 * h + 128)
                r = 8 * t + i
                block = flat[pl.ds(h * count * rows + r, count, stride=rows), :]
                high = block.astype(jnp.bfloat16)
                out_ref[r, 0:count, cols] = high
                out_ref[r, count : 2 * count, cols] = (block - high.astype(jnp.float32)).astype(jnp.bfloat16)
            return carry

        lax.fori_loop(0, 8, split, 0, unroll=4)


def product(x_ref, y_ref, s_refs):
    def group(s_ref, first):
        def body(t, carry):
            total = None
            for k in range(16):
                r = 16 * t + k
                block = jnp.concatenate([x_ref[first + r], y_ref[first + r]], 0)
                high = block.astype(jnp.bfloat16)
                low = (block - high.astype(jnp.float32)).astype(jnp.bfloat16)
                one = lax.dot_general(
                    jnp.concatenate([high, low], 0),
                    s_ref[r],
                    (((1,), (1,)), ((), ())),
                    preferred_element_type=jnp.float32,
                )
                total = one if total is None else total + one
            return carry + total

        return body

    whole = jnp.zeros((64, 128), jnp.float32)
    for k, s_ref in enumerate(s_refs):
        whole = lax.fori_loop(0, ROWS // 32, group(s_ref, k * ROWS // 2), whole)
    rows = whole[0:32, :] + whole[32:64, :]
    return rows[:, 0:64] + rows[:, 64:128]


def first_gram_kernel(x_ref, y_ref, s0_ref, s1_ref, out_ref):
    out_ref[...] = product(x_ref, y_ref, (s0_ref, s1_ref))


def second_gram_kernel(x_ref, y_ref, s0_ref, s1_ref, other_ref, out_ref):
    both = jnp.concatenate([other_ref[...], product(x_ref, y_ref, (s0_ref, s1_ref))], 1)
    for k in range(out_ref.shape[0]):
        out_ref[k] = both


def spread_kernel(x_ref, out_ref):
    total = jnp.sum(x_ref[...], 0)
    for k in range(out_ref.shape[0]):
        out_ref[k] = total


def finish_kernel(scale, x_ref, out_ref):
    own = lax.axis_index("blk")
    total = jnp.sum(x_ref[...], 0)
    for k in range(4):
        block = own ^ k
        cols = slice(64 * (k // 2), 64 * (k // 2) + 64)
        for s in range(2):
            rows = 16 * (k % 2) + 8 * s
            value = total[rows : rows + 8, cols] * (scale if s == 0 else 0.5 * scale)
            out_ref[s, pl.ds(pl.multiple_of(8 * block, 8), 8), :] = value


def floats(*shape):
    return jax.ShapeDtypeStruct(shape, jnp.float32)


def edges(block_vectors, onsite, mask):
    return pl.pallas_call(
        edges_kernel,
        name="edges",
        out_shape=tuple(floats(10, 8, 128) for _ in range(4)),
        in_specs=[HBM] * 3,
        out_specs=(VMEM,) * 4,
        scratch_shapes=[
            pltpu.VMEM((VECS, ROWS, COLS), jnp.float32),
            pltpu.VMEM((ROWS, COLS), jnp.float32),
            pltpu.VMEM((ROWS, COLS), jnp.int32),
            pltpu.SemaphoreType.DMA((3,)),
        ],
        compiler_params=limit(4),
    )(*(pltpu.with_memory_space_constraint(x, pltpu.HBM) for x in (block_vectors, onsite, mask)))


def filtering(coefs, vectors, mask, vec_strips, onsite=None, coef_strips=None, prepared=None):
    own = prepared is None
    wide = (EXT, VECS, WIDE)
    result = floats(ROWS, 2 * VECS, COLS)
    vector_specs = [
        SMEM,
        pl.BlockSpec((VECS, ROWS, 128), lambda t: (0, 0, 0)),
        pl.BlockSpec((VECS, ROWS, 128), lambda t: (0, 0, 1)),
    ]
    if own:
        operands = (coefs, vectors, vectors, onsite, mask, vec_strips, coef_strips)
    else:
        operands = (coefs, vectors, vectors, mask, vec_strips) + tuple(prepared)
    return pl.pallas_call(
        own_kernel if own else far_kernel,
        name="own" if own else "far",
        grid=(1,),
        out_shape=(result, floats(*wide), floats(*wide)) if own else result,
        in_specs=vector_specs + [VMEM] * 4,
        out_specs=(VMEM,) * 3 if own else VMEM,
        scratch_shapes=[pltpu.VMEM(wide, jnp.float32)] * 3,
        compiler_params=limit(18),
    )(*operands)


def parts(search, half):
    count = search.shape[0]
    rows = ROWS // 2
    return pl.pallas_call(
        functools.partial(parts_kernel, half * rows),
        name="parts",
        out_shape=jax.ShapeDtypeStruct((rows, 2 * count, COLS), jnp.bfloat16),
        in_specs=[HBM],
        out_specs=VMEM,
        scratch_shapes=[
            pltpu.VMEM((2, count, rows, 128), jnp.float32),
            pltpu.SemaphoreType.DMA((rows // 8, 2)),
        ],
        compiler_params=limit(10),
    )(pltpu.with_memory_space_constraint(search, pltpu.HBM))


def small(kernel, shape, limited, *operands):
    return pl.pallas_call(
        kernel,
        out_shape=floats(*shape),
        in_specs=[VMEM] * len(operands),
        out_specs=VMEM,
        compiler_params=limit(limited),
    )(*operands)


def limit(mib):
    return pltpu.CompilerParams(vmem_limit_bytes=mib << 20)


def shifted(block, axis, by):
    count = lax.axis_size(axis)
    return lax.ppermute(block, axis, [(i, i + by) for i in range(count) if 0 <= i + by < count])


def strips(above_below, picks):
    return [f[low:high] for f in above_below for low, high in picks]


def program(block_vectors, search_vectors, onsite_energy, site_mask, filter_coefs):
    across = [(0, 2), (1, 3), (2, 0), (3, 1)]
    swap = [(0, 1), (1, 0), (2, 3), (3, 2)]
    left, right, up, down = edges(block_vectors, onsite_energy, site_mask)
    from_left = shifted(right, "ly", 1)
    from_right = shifted(left, "ly", -1)
    far_vectors = lax.ppermute(block_vectors, "blk", across)
    split_low = parts(search_vectors, 0)
    slot = lax.broadcasted_iota(jnp.int32, (10, 8, 128), 2) // GROUP
    up = jnp.concatenate([up, jnp.where(slot == 0, from_left, from_right)], 0)
    from_below = shifted(up, "lx", -1)
    down = jnp.concatenate([down, jnp.where(slot == TILES - 1, from_left, from_right)], 0)
    from_above = shifted(down, "lx", 1)
    split_high = parts(search_vectors, 1)
    outer = (from_above, from_below)
    vec_strips = jnp.concatenate([from_left[:8], from_right[:8]] + strips(outer, ((0, 6), (10, 18))), 0)
    coef_strips = jnp.concatenate([from_left[8:], from_right[8:]] + strips(outer, ((6, 10), (18, 20))), 0)
    far_strips = lax.ppermute(vec_strips, "blk", across)
    own, *prepared = filtering(
        filter_coefs, block_vectors, site_mask, vec_strips, onsite_energy, coef_strips
    )
    own_near = lax.ppermute(own, "blk", swap)
    far = filtering(filter_coefs, far_vectors, site_mask, far_strips, prepared=prepared)
    far_near = lax.ppermute(far, "blk", swap)
    first = small(first_gram_kernel, (32, 64), 20, own, own_near, split_low, split_high)
    count = lax.axis_size("ly")
    copies = small(second_gram_kernel, (count, 32, 128), 20, far, far_near, split_low, split_high, first)
    copies = lax.all_to_all(copies, "ly", 0, 0)
    copies = small(spread_kernel, (lax.axis_size("lx"), 32, 128), 2, copies)
    copies = lax.all_to_all(copies, "lx", 0, 0)
    nrows, ncols = onsite_energy.shape
    scale = 1.0 / math.sqrt(nrows * ncols * lax.axis_size("lx") * lax.axis_size("ly"))
    return small(functools.partial(finish_kernel, scale), (2, 4 * VECS, 64), 2, copies)


def solution(mesh):
    placed = (P("blk", "lx", "ly"), P("blk", "lx", "ly"), P("lx", "ly"), P("lx", "ly"), P())
    return jax.shard_map(program, mesh=mesh, in_specs=placed, out_specs=P(None, None, "blk"), check_vma=False)
```

time: 107 us -> 105 us (0.981)
  blocking collectives: 12.3 us -> 30 us
  starting transfers between devices: 23.6 us -> 13.4 us
  local copies, waits for them, and re-layouts: 8.41 us -> 0.05 us
  Pallas kernels: 33.2 us -> 38 us
  waiting for transfers between devices: 28.1 us -> 23.5 us
    ppermute x4, waiting for transfers between devices: 4.58 us -> 23.5 us  [shifted(): lax.ppermute(block, axis, [(i, i + by) for i in range(count) if 0 <= i +...]
    all_to_all x1 -> x2, blocking collectives: 12.3 us -> 30 us  [the longest x1 17.2 us: program(): copies = lax.all_to_all(copies, 'lx', 0, 0)]
    ppermute x4, waiting for transfers between devices: 14.5 us -> 0.01 us  [the longest x1 0.01 us: program(): far_vectors = lax.ppermute(block_vectors, 'blk', across)]
    all_to_all x1 -> x0, starting transfers between devices: 10.1 us -> none  [copies_sum(): return lax.all_to_all(copies, axis, 0, 0).sum(0)]
    all_to_all x1 -> x0, waiting for transfers between devices: 9.05 us -> none  [copies_sum(): return lax.all_to_all(copies, axis, 0, 0).sum(0)]
    unnamed x30 -> x18, local copies, waits for them, and re-layouts: 6.46 us -> 0.05 us
    pallas_call x5 -> x8, Pallas kernels: 32.3 us -> 35.8 us  [the longest x2 17.1 us: filtering(): pl.pallas_call(own_kernel if own else far_kernel, name='own' if own else...]
    pallas_call x1, Pallas kernels: 0.93 us -> 2.22 us  [edges(): pl.pallas_call(edges_kernel, name='edges', out_shape=tuple((floats(10, 8,...]
  transfers between devices with their start and end apart: 9 -> 8, of which waited for: 5 -> 4; matrix products, arithmetic and copies ran while one was open for 0% -> 0% of each run, Pallas kernels for 27% -> 32%
where the time goes in v3:
time: 105 us
  Pallas kernels  38 us (36%)
  blocking collectives  30 us (29%)
  waiting for transfers between devices  23.5 us (22%)
  starting transfers between devices  13.4 us (13%)
    ppermute x4, waiting for transfers between devices, shifted(): lax.ppermute(block, axis, [(i, i + by) for i in range(count) if 0 <= i +...  23.5 us
    all_to_all x1, blocking collectives, program(): copies = lax.all_to_all(copies, 'lx', 0, 0)  17.2 us
    pallas_call x2, Pallas kernels, filtering(): pl.pallas_call(own_kernel if own else far_kernel, name='own' if own else...  17.1 us
    all_to_all x1, blocking collectives, program(): copies = lax.all_to_all(copies, 'ly', 0, 0)  12.8 us
    pallas_call x2, Pallas kernels, parts(): pl.pallas_call(functools.partial(parts_kernel, half * rows), name='parts'...  10.1 us
    ppermute x4, starting transfers between devices, shifted(): lax.ppermute(block, axis, [(i, i + by) for i in range(count) if 0 <= i +...  8.81 us
    pallas_call x4, Pallas kernels, small(): pl.pallas_call(kernel, out_shape=floats(*shape), in_specs=[VMEM] * len(op...  8.6 us
    pallas_call x1, Pallas kernels, edges(): pl.pallas_call(edges_kernel, name='edges', out_shape=tuple((floats(10, 8,...  2.22 us
  transfers between devices with their start and end apart: 8, of which 4 were waited for; matrix products, arithmetic and copies ran while one was open for 0% of the time, Pallas kernels for 32%

profile of v3, /device:TPU:16, one launch (start us, length us, event | category | flops | bytes accessed | tf_op | source)
XLA Modules:
  0.0 105.1 jit_solution(16999373918686529048)
XLA Ops:
  0.0 2.1 %collective-permute-start = (f32[8,128,256]{2,1,0:T(8,128)}, f32[8,128,256]{2,1,0:T(8,128)S(1)}, u32[]{:S(2)}, u32[]{:S(2)}) collective-permute-start(f32[8,128,256]{2,1,0:T(8,128)} %v1_ref.1), channel_id=1, source_target_pairs={{0,2},{1,3},{2,0},{3,1},{4,6},{5,7},{6,4},{7,5},{8,10},{9,11},{10,... | collective-permute-start | bytes 3145736 | tf_op jit(solution)/shard_map/ppermute | solution.py:396
  2.1 2.2 %edges.1 = (f32[10,8,128]{2,1,0:T(8,128)S(1)}, f32[10,8,128]{2,1,0:T(8,128)S(1)}, f32[10,8,128]{2,1,0:T(8,128)S(1)}, f32[10,8,128]{2,1,0:T(8,128)S(1)}) custom-call(f32[8,128,256]{2,1,0:T(8,128)} %v1_ref.1, f32[128,256]{1,0:T(8,128)} %onsite_ref.1, s32[128,256]{1,0:T(8,128)} %mask_ref.3), custom_call_target="tpu_custom_call" | custom-call | tf_op jit(solution)/shard_map/edges/pallas_call | solution.py:309
  4.4 2.4 %collective-permute-start.1 = (f32[10,8,128]{2,1,0:T(8,128)S(1)}, f32[10,8,128]{2,1,0:T(8,128)S(1)}, u32[]{:S(2)}, u32[]{:S(2)}) collective-permute-start(f32[10,8,128]{2,1,0:T(8,128)S(1)} %get-tuple-element.12), channel_id=1, source_target_pairs={{0,4},{4,8},{8,12},{12,16},{16,20},{20,24},{24,28},{1,5},{5,9},{9,... | collective-permute-start | bytes 122888 | tf_op jit(solution)/shard_map/ppermute | solution.py:383
  6.8 1.3 %collective-permute-start.2 = (f32[10,8,128]{2,1,0:T(8,128)S(1)}, f32[10,8,128]{2,1,0:T(8,128)S(1)}, u32[]{:S(2)}, u32[]{:S(2)}) collective-permute-start(f32[10,8,128]{2,1,0:T(8,128)S(1)} %get-tuple-element.13), channel_id=1, source_target_pairs={{4,0},{8,4},{12,8},{16,12},{20,16},{24,20},{28,24},{5,1},{9,5},{13... | collective-permute-start | bytes 122888 | tf_op jit(solution)/shard_map/ppermute | solution.py:383
  8.1 16.7 %collective-permute-done.1 = f32[10,8,128]{2,1,0:T(8,128)S(1)} collective-permute-done((f32[10,8,128]{2,1,0:T(8,128)S(1)}, f32[10,8,128]{2,1,0:T(8,128)S(1)}, u32[]{:S(2)}, u32[]{:S(2)}) %collective-permute-start.1) | collective-permute-done | bytes 40992 | tf_op jit(solution)/shard_map/ppermute | solution.py:383
  24.8 1.8 %collective-permute-done.2 = f32[10,8,128]{2,1,0:T(8,128)S(1)} collective-permute-done((f32[10,8,128]{2,1,0:T(8,128)S(1)}, f32[10,8,128]{2,1,0:T(8,128)S(1)}, u32[]{:S(2)}, u32[]{:S(2)}) %collective-permute-start.2) | collective-permute-done | bytes 40992 | tf_op jit(solution)/shard_map/ppermute | solution.py:383
  26.6 3.8 %collective-permute-start.3 = (f32[20,8,128]{2,1,0:T(8,128)S(1)}, f32[20,8,128]{2,1,0:T(8,128)S(1)}, u32[]{:S(2)}, u32[]{:S(2)}) collective-permute-start(f32[20,8,128]{2,1,0:T(8,128)S(1)} %pad_maximum_fusion), channel_id=1, source_target_pairs={{0,32},{32,64},{64,96},{96,128},{128,160},{160,192},{192,224},{1,3... | collective-permute-start | bytes 245768 | tf_op jit(solution)/shard_map/ppermute | solution.py:383
  30.5 1.3 %collective-permute-start.4 = (f32[20,8,128]{2,1,0:T(8,128)S(1)}, f32[20,8,128]{2,1,0:T(8,128)S(1)}, u32[]{:S(2)}, u32[]{:S(2)}) collective-permute-start(f32[20,8,128]{2,1,0:T(8,128)S(1)} %pad_maximum_fusion.1), channel_id=1, source_target_pairs={{32,0},{64,32},{96,64},{128,96},{160,128},{192,160},{224,192},{33,... | collective-permute-start | bytes 245768 | tf_op jit(solution)/shard_map/ppermute | solution.py:383
  31.8 0.7 collective-permute-done.3
  32.5 4.3 %collective-permute-done.4 = f32[20,8,128]{2,1,0:T(8,128)S(1)} collective-permute-done((f32[20,8,128]{2,1,0:T(8,128)S(1)}, f32[20,8,128]{2,1,0:T(8,128)S(1)}, u32[]{:S(2)}, u32[]{:S(2)}) %collective-permute-start.4) | collective-permute-done | bytes 81952 | tf_op jit(solution)/shard_map/ppermute | solution.py:383
  36.8 1.8 %collective-permute-start.5 = (f32[44,8,128]{2,1,0:T(8,128)S(1)}, f32[44,8,128]{2,1,0:T(8,128)S(1)}, u32[]{:S(2)}, u32[]{:S(2)}) collective-permute-start(f32[44,8,128]{2,1,0:T(8,128)S(1)} %slice_dynamic-update-slice_fusion.vec_ref), channel_id=1, source_target_pairs={{0,2},{1,3},{2,0},{3,1},{4,6},{5,7},{6,4},{7,5},{8,10},{9,11},{10,... | collective-permute-start | bytes 540680 | tf_op jit(solution)/shard_map/ppermute | solution.py:407
  38.6 8.7 %own.1 = (f32[128,16,256]{2,1,0:T(8,128)S(1)}, f32[136,8,384]{2,1,0:T(8,128)S(1)}, f32[136,8,384]{2,1,0:T(8,128)S(1)}) custom-call(f32[5]{0:T(128)S(1)} %copy-done.3, f32[8,128,256]{2,1,0:T(8,128)S(1)} %copy-done, f32[8,128,256]{2,1,0:T(8,128)S(1)} %copy-done, f32[128,256]{1,0:T(8,128)S(1)} %copy-done.2, s32[128,256]{1,0:T(8,128)S(1)} %copy-done.1, ...), custom_call_target="tpu_custom_call" | custom-call | tf_op jit(solution)/shard_map/own/pallas_call | solution.py:338
  47.4 0.1 collective-permute-start.7
  47.5 0.0 collective-permute-done.5.vec_ref
  47.5 0.0 collective-permute-done.v0_ref.v1_ref
  47.5 8.3 %far.1.x_ref = f32[128,16,256]{2,1,0:T(8,128)S(1)} custom-call(f32[5]{0:T(128)S(1)} %copy-done.3, f32[8,128,256]{2,1,0:T(8,128)S(1)} %collective-permute-done.v0_ref.v1_ref, f32[8,128,256]{2,1,0:T(8,128)S(1)} %collective-permute-done.v0_ref.v1_ref, s32[128,256]{1,0:T(8,128)S(1)} %copy-done.1, f32[44,8,128]{2,1,0:T(8,128)S(1)} %collective-permute-done.5.vec_ref, ...), custom_call_target="tpu_custom_call" | custom-call | tf_op jit(solution)/shard_map/far/pallas_call | solution.py:338
  55.8 0.6 collective-permute-start.6
  56.4 5.1 %parts.2.s0_ref = bf16[64,128,256]{2,1,0:T(8,128)(2,1)S(1)} custom-call(f32[64,128,256]{2,1,0:T(8,128)} %s_hbm.3), custom_call_target="tpu_custom_call" | custom-call | tf_op jit(solution)/shard_map/parts/pallas_call | solution.py:353
  61.5 5.1 %parts.3.s1_ref = bf16[64,128,256]{2,1,0:T(8,128)(2,1)S(1)} custom-call(f32[64,128,256]{2,1,0:T(8,128)} %s_hbm.3), custom_call_target="tpu_custom_call" | custom-call | tf_op jit(solution)/shard_map/parts/pallas_call | solution.py:353
  66.6 3.9 %shard_map.55.other_ref = f32[32,64]{1,0:T(8,128)S(1)} custom-call(f32[128,16,256]{2,1,0:T(8,128)S(1)} %get-tuple-element.18.x_ref, f32[128,16,256]{2,1,0:T(8,128)S(1)} %collective-permute-done.7.y_ref, bf16[64,128,256]{2,1,0:T(8,128)(2,1)S(1)} %parts.2.s0_ref, bf16[64,128,256]{2,1,0:T(8,128)(2,1)S(1)} %parts.3.s1_ref), custom_call_target="tpu_custom_call" | custom-call | tf_op jit(solution)/shard_map/pallas_call | solution.py:368
  70.5 4.0 %shard_map.56 = f32[8,32,128]{2,1,0:T(8,128)S(1)} custom-call(f32[128,16,256]{2,1,0:T(8,128)S(1)} %far.1.x_ref, f32[128,16,256]{2,1,0:T(8,128)S(1)} %collective-permute-done.6.y_ref, bf16[64,128,256]{2,1,0:T(8,128)(2,1)S(1)} %parts.2.s0_ref, bf16[64,128,256]{2,1,0:T(8,128)(2,1)S(1)} %parts.3.s1_ref, f32[32,64]{1,0:T(8,128)S(1)} %shard_map.55.other_ref), custom_call_target="tpu_custom_call" | custom-call | tf_op jit(solution)/shard_map/pallas_call | solution.py:368
  74.5 12.8 %all_to_all.10.x_ref = f32[8,32,128]{2,1,0:T(8,128)S(1)} all-to-all(f32[8,32,128]{2,1,0:T(8,128)S(1)} %shard_map.56), channel_id=1, replica_groups=mesh['lx'=8,'ly'=8,'blk'=4] {'ly'}, dimensions={0} | all-to-all | bytes 262144 | tf_op jit(solution)/shard_map/all_to_all | solution.py:417
  87.3 17.2 %all_to_all.11.x_ref = f32[8,32,128]{2,1,0:T(8,128)S(1)} all-to-all(f32[8,32,128]{2,1,0:T(8,128)S(1)} %shard_map.57), channel_id=1, replica_groups=mesh['lx'=8,'ly'=8,'blk'=4] {'lx'}, dimensions={0} | all-to-all | bytes 262144 | tf_op jit(solution)/shard_map/all_to_all | solution.py:419
  104.4 0.7 shard_map.58
  (28 shorter events, 0.1 us)
Async XLA Ops:
  0.0 38.6 %copy-start = (f32[8,128,256]{2,1,0:T(8,128)S(1)}, f32[8,128,256]{2,1,0:T(8,128)}, u32[]{:S(2)}) copy-start(f32[8,128,256]{2,1,0:T(8,128)} %v1_ref.1) | copy-start | bytes 3145732
  0.0 38.6 %copy-start.2 = (f32[128,256]{1,0:T(8,128)S(1)}, f32[128,256]{1,0:T(8,128)}, u32[]{:S(2)}) copy-start(f32[128,256]{1,0:T(8,128)} %onsite_ref.1) | copy-start | bytes 393220
  0.0 38.6 %copy-start.1 = (s32[128,256]{1,0:T(8,128)S(1)}, s32[128,256]{1,0:T(8,128)}, u32[]{:S(2)}) copy-start(s32[128,256]{1,0:T(8,128)} %mask_ref.3) | copy-start | bytes 393220
  0.0 38.6 %copy-start.3 = (f32[5]{0:T(128)S(1)}, f32[5]{0:T(128)}, u32[]{:S(2)}) copy-start(f32[5]{0:T(128)} %c_ref.3) | copy-start | bytes 64
  0.0 47.5 %collective-permute-start = (f32[8,128,256]{2,1,0:T(8,128)}, f32[8,128,256]{2,1,0:T(8,128)S(1)}, u32[]{:S(2)}, u32[]{:S(2)}) collective-permute-start(f32[8,128,256]{2,1,0:T(8,128)} %v1_ref.1), channel_id=1, source_target_pairs={{0,2},{1,3},{2,0},{3,1},{4,6},{5,7},{6,4},{7,5},{8,10},{9,11},{10,... | collective-permute-start | bytes 3145736 | tf_op jit(solution)/shard_map/ppermute | solution.py:396
  4.4 20.4 %collective-permute-start.1 = (f32[10,8,128]{2,1,0:T(8,128)S(1)}, f32[10,8,128]{2,1,0:T(8,128)S(1)}, u32[]{:S(2)}, u32[]{:S(2)}) collective-permute-start(f32[10,8,128]{2,1,0:T(8,128)S(1)} %get-tuple-element.12), channel_id=1, source_target_pairs={{0,4},{4,8},{8,12},{12,16},{16,20},{20,24},{24,28},{1,5},{5,9},{9,... | collective-permute-start | bytes 122888 | tf_op jit(solution)/shard_map/ppermute | solution.py:383
  6.8 19.8 %collective-permute-start.2 = (f32[10,8,128]{2,1,0:T(8,128)S(1)}, f32[10,8,128]{2,1,0:T(8,128)S(1)}, u32[]{:S(2)}, u32[]{:S(2)}) collective-permute-start(f32[10,8,128]{2,1,0:T(8,128)S(1)} %get-tuple-element.13), channel_id=1, source_target_pairs={{4,0},{8,4},{12,8},{16,12},{20,16},{24,20},{28,24},{5,1},{9,5},{13... | collective-permute-start | bytes 122888 | tf_op jit(solution)/shard_map/ppermute | solution.py:383
  26.6 5.9 %collective-permute-start.3 = (f32[20,8,128]{2,1,0:T(8,128)S(1)}, f32[20,8,128]{2,1,0:T(8,128)S(1)}, u32[]{:S(2)}, u32[]{:S(2)}) collective-permute-start(f32[20,8,128]{2,1,0:T(8,128)S(1)} %pad_maximum_fusion), channel_id=1, source_target_pairs={{0,32},{32,64},{64,96},{96,128},{128,160},{160,192},{192,224},{1,3... | collective-permute-start | bytes 245768 | tf_op jit(solution)/shard_map/ppermute | solution.py:383
  30.5 6.3 %collective-permute-start.4 = (f32[20,8,128]{2,1,0:T(8,128)S(1)}, f32[20,8,128]{2,1,0:T(8,128)S(1)}, u32[]{:S(2)}, u32[]{:S(2)}) collective-permute-start(f32[20,8,128]{2,1,0:T(8,128)S(1)} %pad_maximum_fusion.1), channel_id=1, source_target_pairs={{32,0},{64,32},{96,64},{128,96},{160,128},{192,160},{224,192},{33,... | collective-permute-start | bytes 245768 | tf_op jit(solution)/shard_map/ppermute | solution.py:383
  36.8 10.7 %collective-permute-start.5 = (f32[44,8,128]{2,1,0:T(8,128)S(1)}, f32[44,8,128]{2,1,0:T(8,128)S(1)}, u32[]{:S(2)}, u32[]{:S(2)}) collective-permute-start(f32[44,8,128]{2,1,0:T(8,128)S(1)} %slice_dynamic-update-slice_fusion.vec_ref), channel_id=1, source_target_pairs={{0,2},{1,3},{2,0},{3,1},{4,6},{5,7},{6,4},{7,5},{8,10},{9,11},{10,... | collective-permute-start | bytes 540680 | tf_op jit(solution)/shard_map/ppermute | solution.py:407
  47.4 19.2 %collective-permute-start.7 = (f32[128,16,256]{2,1,0:T(8,128)S(1)}, f32[128,16,256]{2,1,0:T(8,128)S(1)}, u32[]{:S(2)}, u32[]{:S(2)}) collective-permute-start(f32[128,16,256]{2,1,0:T(8,128)S(1)} %get-tuple-element.18.x_ref), channel_id=1, source_target_pairs={{0,1},{1,0},{2,3},{3,2},{4,5},{5,4},{6,7},{7,6},{8,9},{9,8},{10,11... | collective-permute-start | bytes 6291464 | tf_op jit(solution)/shard_map/ppermute | solution.py:411
  55.8 14.6 %collective-permute-start.6 = (f32[128,16,256]{2,1,0:T(8,128)S(1)}, f32[128,16,256]{2,1,0:T(8,128)S(1)}, u32[]{:S(2)}, u32[]{:S(2)}) collective-permute-start(f32[128,16,256]{2,1,0:T(8,128)S(1)} %far.1.x_ref), channel_id=1, source_target_pairs={{0,1},{1,0},{2,3},{3,2},{4,5},{5,4},{6,7},{7,6},{8,9},{9,8},{10,11... | collective-permute-start | bytes 6291464 | tf_op jit(solution)/shard_map/ppermute | solution.py:413
